TPU v7x, 512 devices: a whole 4x8x8 slice. The times are simulated.
512 devices in a mesh: gx: 8 (over x, y_hi), gy: 8 (over z), gz: 8 (over y_lo, core).
Axes of the slice: x: 4, y: 8 (y_hi: 2, y_lo: 4; y = y_hi * 4 + y_lo), z: 8, core: 2. Of those that a mesh axis runs over, the one named last changes fastest.
Arguments:
- orbitals: float32 [128, 128, 128, 64], P('gx', 'gy', 'gz'), may hold values from -6 to 6
- potential: float32 [128, 128, 128], P('gx', 'gy', 'gz'), may hold values from -1.5 to 1
Outputs:
- basis: float32 [128, 128, 128, 64], P('gx', 'gy', 'gz')
- blocks: float32 [8, 8, 8, 7, 64, 64], P('gx', 'gy', 'gz')
All inputs are finite; a program needn't handle non-finite values.
Results may differ from a plain program's by a relative error of at most 0.0003.
Values sent between devices are 32-bit elements; how exact they have to be, the bound alone decides.
A program may use at most 128 MiB of HBM per device.

v0:
```python
import jax
import jax.numpy as jnp
import numpy as np
from jax import lax
from jax.sharding import PartitionSpec as P

BUF = 3


PENALTY = 2.0
LOW_BOUND = -1.5
CUTOFF = 8.0
HIGH_BOUND = 16.0


def extended(cells, sides, width):
    for axis, dim in sides:
        count = lax.axis_size(axis)
        head = lax.slice_in_dim(cells, 0, width, axis=dim)
        tail = lax.slice_in_dim(cells, cells.shape[dim] - width, cells.shape[dim], axis=dim)
        cells = jnp.concatenate(
            [
                lax.ppermute(tail, axis, [(i, (i + 1) % count) for i in range(count)]),
                cells,
                lax.ppermute(head, axis, [((i + 1) % count, i) for i in range(count)]),
            ],
            axis=dim,
        )
    return cells


def spectral_tables(points):
    indices = np.arange(points)
    offsets = indices[:, None] - indices[None, :]
    nyquist = points // 2
    deriv_one = np.zeros((points, points))
    deriv_two = np.zeros((points, points))
    for harmonic in range(1, nyquist):
        wavenum = 2.0 * np.pi * harmonic / points
        deriv_one = deriv_one - 2.0 * wavenum * np.sin(wavenum * offsets) / points
        deriv_two = deriv_two - 2.0 * wavenum * wavenum * np.cos(wavenum * offsets) / points
    deriv_two = deriv_two - np.pi * np.pi * np.cos(np.pi * offsets) / points
    return (jnp.asarray(deriv_one, jnp.float32), jnp.asarray(deriv_two, jnp.float32))


def apply_along(matrix, field, axis_pos):
    forms = ("ia,ajko->ijko", "ja,iako->ijko", "ka,ijao->ijko")
    return jnp.einsum(forms[axis_pos], matrix, field, precision=lax.Precision.HIGHEST)


def hamiltonian(field, ext_pot, deriv_two):
    first_len, second_len, third_len, width = field.shape
    flat = field.reshape(first_len, second_len, third_len * width)
    along_x = jnp.einsum("ia,ajk->ijk", deriv_two, flat, precision=lax.Precision.HIGHEST)
    along_y = jnp.einsum("ja,iak->ijk", deriv_two, flat, precision=lax.Precision.HIGHEST)
    laplace = (along_x + along_y).reshape(field.shape) + apply_along(deriv_two, field, 2)
    return -0.5 * laplace + ext_pot[..., None] * field


def chebyshev(start, ext_pot, deriv_two):
    half_width = (HIGH_BOUND - CUTOFF) / 2.0
    center = (HIGH_BOUND + CUTOFF) / 2.0
    scale_now = half_width / (LOW_BOUND - center)
    tau_factor = 2.0 / scale_now
    current = (hamiltonian(start, ext_pot, deriv_two) - center * start) * (scale_now / half_width)
    scale_next = 1.0 / (tau_factor - scale_now)
    applied = hamiltonian(current, ext_pot, deriv_two) - center * current
    following = applied * (2.0 * scale_next / half_width) - scale_now * scale_next * start
    return following


def element_fields(ext_orb, ext_pot, deriv_one, deriv_two, margin, cells):
    filtered = chebyshev(ext_orb, ext_pot, deriv_two)
    stop = margin + cells
    row_block = deriv_one[margin:stop]
    interior = filtered[margin:stop, margin:stop, margin:stop]
    grad_x = apply_along(row_block, filtered[:, margin:stop, margin:stop], 0)
    grad_y = apply_along(row_block, filtered[margin:stop, :, margin:stop], 1)
    grad_z = apply_along(row_block, filtered[margin:stop, margin:stop, :], 2)
    return (interior, grad_x, grad_y, grad_z)


def face_product(left, right):
    return jnp.einsum("...pqi,...pqj->...ij", left, right, precision=lax.Precision.HIGHEST)


def neighbour_block(own_value, own_deriv, other_value, other_deriv, sign):
    skew = face_product(own_deriv, other_value) - face_product(own_value, other_deriv)
    return 0.25 * sign * skew - 0.5 * PENALTY * face_product(own_value, other_value)


def own_face(value, deriv, sign):
    mixed = face_product(value, deriv) + face_product(deriv, value)
    return -0.25 * sign * mixed + 0.5 * PENALTY * face_product(value, value)


def assemble(interior, gradients, pot_el, lowers, uppers):
    volume_form = "...xyzi,...xyzj->...ij"
    diagonal = jnp.einsum(
        volume_form, interior, pot_el[..., None] * interior, precision=lax.Precision.HIGHEST
    )
    for axis_pos in range(3):
        diagonal = diagonal + 0.5 * jnp.einsum(
            volume_form, gradients[axis_pos], gradients[axis_pos], precision=lax.Precision.HIGHEST
        )
    cells = interior.shape[-2]
    coupled = []
    for axis_pos in range(3):
        grid_axis = interior.ndim - 4 + axis_pos
        low_value = jnp.take(interior, 0, axis=grid_axis)
        low_deriv = jnp.take(gradients[axis_pos], 0, axis=grid_axis)
        high_value = jnp.take(interior, cells - 1, axis=grid_axis)
        high_deriv = jnp.take(gradients[axis_pos], cells - 1, axis=grid_axis)
        diagonal = diagonal + own_face(low_value, low_deriv, -1.0)
        diagonal = diagonal + own_face(high_value, high_deriv, 1.0)
        coupled.append(
            neighbour_block(low_value, low_deriv, lowers[axis_pos][0], lowers[axis_pos][1], -1.0)
        )
        coupled.append(
            neighbour_block(high_value, high_deriv, uppers[axis_pos][0], uppers[axis_pos][1], 1.0)
        )
    return jnp.stack([diagonal] + coupled, axis=-3)


def on_device(orbitals, potential):
    ext_orb, ext_pot = (
        extended(orbitals, (("gx", 0), ("gy", 1), ("gz", 2)), BUF),
        extended(potential, (("gx", 0), ("gy", 1), ("gz", 2)), BUF),
    )
    cells = orbitals.shape[0]
    deriv_one, deriv_two = spectral_tables(ext_orb.shape[0])
    interior, grad_x, grad_y, grad_z = element_fields(
        ext_orb, ext_pot, deriv_one, deriv_two, BUF, cells
    )
    gradients = (grad_x, grad_y, grad_z)
    padded_x = (extended(interior, (("gx", 0),), 1), extended(grad_x, (("gx", 0),), 1))
    padded_y = (extended(interior, (("gy", 1),), 1), extended(grad_y, (("gy", 1),), 1))
    padded_z = (extended(interior, (("gz", 2),), 1), extended(grad_z, (("gz", 2),), 1))
    lowers = (
        (padded_x[0][0], padded_x[1][0]),
        (padded_y[0][:, 0], padded_y[1][:, 0]),
        (padded_z[0][:, :, 0], padded_z[1][:, :, 0]),
    )
    uppers = (
        (padded_x[0][-1], padded_x[1][-1]),
        (padded_y[0][:, -1], padded_y[1][:, -1]),
        (padded_z[0][:, :, -1], padded_z[1][:, :, -1]),
    )
    blocks = assemble(interior, gradients, potential, lowers, uppers)
    return (interior, blocks[None, None, None])


def solution(mesh):
    return jax.shard_map(
        on_device,
        mesh=mesh,
        in_specs=(P("gx", "gy", "gz", None), P("gx", "gy", "gz")),
        out_specs=(P("gx", "gy", "gz", None), P("gx", "gy", "gz", None, None, None)),
        check_vma=False,
    )
```

profile of v0, /device:TPU:2, one launch (start us, length us, event | category | flops | bytes accessed | tf_op | source)
XLA Modules:
  0.0 315.9 jit_solution(10801772122866688632)
XLA Ops:
  1.4 7.7 %collective-permute-start.7 = (f32[3,16,16]{2,1,0:T(8,128)S(1)}, f32[3,16,16]{2,1,0:T(8,128)S(1)}, u32[]{:S(2)}, u32[]{:S(2)}) collective-permute-start(f32[3,16,16]{2,1,0:T(8,128)S(1)} %get-tuple-element.98), channel_id=1, source_target_pairs={{64,0},{128,64},{192,128},{256,192},{320,256},{384,320},{448,384},... | collective-permute-start | bytes 9224 | tf_op jit(solution)/shard_map/ppermute | solution.py:25
  12.3 8.6 %collective-permute-start.1 = (f32[3,16,16,64]{3,2,1,0:T(8,128)S(1)}, f32[3,16,16,64]{3,2,1,0:T(8,128)S(1)}, u32[]{:S(2)}, u32[]{:S(2)}) collective-permute-start(f32[3,16,16,64]{3,2,1,0:T(8,128)S(1)} %get-tuple-element.92), channel_id=1, source_target_pairs={{64,0},{128,64},{192,128},{256,192},{320,256},{384,320},{448,384},... | collective-permute-start | bytes 589832 | tf_op jit(solution)/shard_map/ppermute | solution.py:25
  23.8 29.4 %collective-permute-done = f32[3,16,16,64]{3,2,1,0:T(8,128)S(1)} collective-permute-done((f32[3,16,16,64]{3,2,1,0:T(8,128)S(1)}, f32[3,16,16,64]{3,2,1,0:T(8,128)S(1)}, u32[]{:S(2)}, u32[]{:S(2)}) %collective-permute-start) | collective-permute-done | bytes 196640 | tf_op jit(solution)/shard_map/ppermute | solution.py:23
  55.2 4.3 %collective-permute-start.2 = (f32[22,3,16,64]{3,2,1,0:T(8,128)S(1)}, f32[22,3,16,64]{3,2,1,0:T(8,128)S(1)}, u32[]{:S(2)}, u32[]{:S(2)}) collective-permute-start(f32[22,3,16,64]{3,2,1,0:T(8,128)S(1)} %get-tuple-element.84), channel_id=1, source_target_pairs={{0,8},{8,16},{16,24},{24,32},{32,40},{40,48},{48,56},{56,0},{1,9},... | collective-permute-start | bytes 811016 | tf_op jit(solution)/shard_map/ppermute | solution.py:23
  59.5 8.6 %collective-permute-start.3 = (f32[22,3,16,64]{3,2,1,0:T(8,128)S(1)}, f32[22,3,16,64]{3,2,1,0:T(8,128)S(1)}, u32[]{:S(2)}, u32[]{:S(2)}) collective-permute-start(f32[22,3,16,64]{3,2,1,0:T(8,128)S(1)} %get-tuple-element.85), channel_id=1, source_target_pairs={{8,0},{16,8},{24,16},{32,24},{40,32},{48,40},{56,48},{0,56},{9,1},... | collective-permute-start | bytes 811016 | tf_op jit(solution)/shard_map/ppermute | solution.py:25
  70.0 5.1 %collective-permute-start.9 = (f32[22,3,16]{2,1,0:T(4,128)S(1)}, f32[22,3,16]{2,1,0:T(4,128)S(1)}, u32[]{:S(2)}, u32[]{:S(2)}) collective-permute-start(f32[22,3,16]{2,1,0:T(4,128)S(1)} %get-tuple-element.97), channel_id=1, source_target_pairs={{8,0},{16,8},{24,16},{32,24},{40,32},{48,40},{56,48},{0,56},{9,1},... | collective-permute-start | bytes 12680 | tf_op jit(solution)/shard_map/ppermute | solution.py:25
  82.0 8.3 %collective-permute-start.10 = (f32[22,22,3]{2,1,0:T(8,128)S(1)}, f32[22,22,3]{2,1,0:T(8,128)S(1)}, u32[]{:S(2)}, u32[]{:S(2)}) collective-permute-start(f32[22,22,3]{2,1,0:T(8,128)S(1)} %get-tuple-element.94), channel_id=1, source_target_pairs={{0,1},{1,2},{2,3},{3,4},{4,5},{5,6},{6,7},{7,0},{8,9},{9,10},{10,1... | collective-permute-start | bytes 17432 | tf_op jit(solution)/shard_map/ppermute | solution.py:23
  92.3 16.9 %collective-permute-done.10 = f32[22,22,3]{2,1,0:T(8,128)S(1)} collective-permute-done((f32[22,22,3]{2,1,0:T(8,128)S(1)}, f32[22,22,3]{2,1,0:T(8,128)S(1)}, u32[]{:S(2)}, u32[]{:S(2)}) %collective-permute-start.10) | collective-permute-done | bytes 5840 | tf_op jit(solution)/shard_map/ppermute | solution.py:23
  122.8 5.0 %convolution_add_fusion.1 = f32[22,22,1408]{2,0,1:T(8,128)} fusion(f32[22,22,1]{1,0,2:T(8,128)S(1)} %copy-done.8, f32[22,22,1408]{2,1,0:T(8,128)S(1)} %reshape.255, f32[22,1408,22]{1,2,0:T(8,128)S(1)} %fusion.144), kind=kOutput, calls=%fused_computation.12 | convolution fusion | flops 180590080 | bytes 8179600 | tf_op jit(solution)/shard_map/ia,ajk->ijk/dot_general | solution.py:54
  127.8 5.6 %reshape.25 = f32[22,22,22,64]{3,2,0,1:T(8,128)} reshape(f32[22,22,1408]{2,0,1:T(8,128)} %convolution_add_fusion.1) | data formatting | bytes 5451776 | tf_op jit(solution)/shard_map/reshape | solution.py:56
  133.4 15.4 %broadcast_multiply_fusion = (f32[22,22,22,64]{3,2,1,0:T(8,128)}, f32[22,22,22,64]{3,2,1,0:T(8,128)}) fusion(f32[22,22,3,64]{3,2,1,0:T(4,128)} %copy-done.4, f32[22,3,16,64]{3,2,1,0:T(8,128)} %copy-done.6, f32[22,16,16,64]{3,2,1,0:T(8,128)S(1)} %copy-done.2, f32[22,3,16,64]{3,2,1,0:T(8,128)S(1)} %collective-permute-done.2, f32[22,22,3,64]{3,2,1,0:T(4,128)} %copy-done.5, ...), kind=kOutput, calls=%fused_computation.21 | convolution fusion | flops 190130688 | bytes 10948080 | tf_op jit(solution)/shard_map/ka,ijao->ijko/dot_general | solution.py:48
  148.8 4.3 %reshape.26 = f32[22,22,1408]{2,1,0:T(8,128)S(1)} reshape(f32[22,22,22,64]{3,2,1,0:T(8,128)} %get-tuple-element.100) | data formatting | bytes 5451776 | tf_op jit(solution)/shard_map/reshape | solution.py:53
  161.4 5.6 %reshape.27 = f32[22,22,22,64]{3,2,1,0:T(8,128)} reshape(f32[22,22,1408]{2,1,0:T(8,128)} %copy.29) | data formatting | bytes 5451776 | tf_op jit(solution)/shard_map/reshape | solution.py:56
  167.0 15.9 %fusion.4 = f32[22,22,22,64]{3,2,1,0:T(8,128)S(1)} fusion(f32[22,22,22,64]{3,2,1,0:T(8,128)} %reshape.27, f32[22,22,22,64]{3,2,1,0:T(8,128)} %get-tuple-element.101, f32[22,22,22]{2,1,0:T(8,128)} %get-tuple-element.74, f32[22,22,1,1]{1,0,3,2:T(8,128)S(1)} %copy-done.11, f32[22,22,3,64]{3,2,1,0:T(4,128)} %copy-done.4, f32[22,3,16,64]{3,2,1,0:T(8,128)} %copy-done.6, ...), kind=kOutput, calls=%fused_computation.6 | convolution fusion | flops 189449216 | bytes 10948080 | tf_op jit(solution)/shard_map/ka,ijao->ijko/dot_general | solution.py:48
  188.9 4.6 %collective-permute-start.22 = (f32[16,16,1,64]{3,2,1,0:T(1,128)S(1)}, f32[16,16,1,64]{3,2,1,0:T(1,128)S(1)}, u32[]{:S(2)}, u32[]{:S(2)}) collective-permute-start(f32[16,16,1,64]{3,2,1,0:T(1,128)S(1)} %get-tuple-element.80), channel_id=1, source_target_pairs={{1,0},{2,1},{3,2},{4,3},{5,4},{6,5},{7,6},{0,7},{9,8},{10,9},{11,1... | collective-permute-start | bytes 196616 | tf_op jit(solution)/shard_map/ppermute | solution.py:25
  198.6 5.6 %collective-permute-start.23 = (f32[16,16,1,64]{3,2,1,0:T(1,128)S(1)}, f32[16,16,1,64]{3,2,1,0:T(1,128)S(1)}, u32[]{:S(2)}, u32[]{:S(2)}) collective-permute-start(f32[16,16,1,64]{3,2,1,0:T(1,128)S(1)} %get-tuple-element.90), channel_id=1, source_target_pairs={{1,0},{2,1},{3,2},{4,3},{5,4},{6,5},{7,6},{0,7},{9,8},{10,9},{11,1... | collective-permute-start | bytes 196616 | tf_op jit(solution)/shard_map/ppermute | solution.py:25
  212.4 5.8 %collective-permute-start.19 = (f32[16,1,16,64]{3,1,2,0:T(1,128)S(1)}, f32[16,1,16,64]{3,1,2,0:T(1,128)S(1)}, u32[]{:S(2)}, u32[]{:S(2)}) collective-permute-start(f32[16,1,16,64]{3,1,2,0:T(1,128)S(1)} %get-tuple-element.88), channel_id=1, source_target_pairs={{8,0},{16,8},{24,16},{32,24},{40,32},{48,40},{56,48},{0,56},{9,1},... | collective-permute-start | bytes 196616 | tf_op jit(solution)/shard_map/ppermute | solution.py:25
  239.0 5.8 %collective-permute-done.17 = f32[16,1,16,64]{3,1,2,0:T(1,128)S(1)} collective-permute-done((f32[16,1,16,64]{3,1,2,0:T(1,128)S(1)}, f32[16,1,16,64]{3,1,2,0:T(1,128)S(1)}, u32[]{:S(2)}, u32[]{:S(2)}) %collective-permute-start.17) | collective-permute-done | bytes 65568 | tf_op jit(solution)/shard_map/ppermute | solution.py:23
  244.8 10.0 %collective-permute-start.15 = (f32[1,16,16,64]{3,0,2,1:T(1,128)S(1)}, f32[1,16,16,64]{3,0,2,1:T(1,128)S(1)}, u32[]{:S(2)}, u32[]{:S(2)}) collective-permute-start(f32[1,16,16,64]{3,0,2,1:T(1,128)S(1)} %get-tuple-element.86), channel_id=1, source_target_pairs={{64,0},{128,64},{192,128},{256,192},{320,256},{384,320},{448,384},... | collective-permute-start | bytes 196616 | tf_op jit(solution)/shard_map/ppermute | solution.py:25
  262.5 9.6 %collective-permute-done.13 = f32[1,16,16,64]{3,0,2,1:T(1,128)S(1)} collective-permute-done((f32[1,16,16,64]{3,0,2,1:T(1,128)S(1)}, f32[1,16,16,64]{3,0,2,1:T(1,128)S(1)}, u32[]{:S(2)}, u32[]{:S(2)}) %collective-permute-start.13) | collective-permute-done | bytes 65568 | tf_op jit(solution)/shard_map/ppermute | solution.py:23
  272.1 6.9 %collective-permute-start.14 = (f32[1,16,16,64]{3,2,1,0:T(8,128)S(1)}, f32[1,16,16,64]{3,2,1,0:T(8,128)S(1)}, u32[]{:S(2)}, u32[]{:S(2)}) collective-permute-start(f32[1,16,16,64]{3,2,1,0:T(8,128)S(1)} %get-tuple-element.78), channel_id=1, source_target_pairs={{64,0},{128,64},{192,128},{256,192},{320,256},{384,320},{448,384},... | collective-permute-start | bytes 196616 | tf_op jit(solution)/shard_map/ppermute | solution.py:25
  279.4 6.3 %collective-permute-done.14 = f32[1,16,16,64]{3,2,1,0:T(8,128)S(1)} collective-permute-done((f32[1,16,16,64]{3,2,1,0:T(8,128)S(1)}, f32[1,16,16,64]{3,2,1,0:T(8,128)S(1)}, u32[]{:S(2)}, u32[]{:S(2)}) %collective-permute-start.14) | collective-permute-done | bytes 65568 | tf_op jit(solution)/shard_map/ppermute | solution.py:25
  288.0 9.4 %collective-permute-done.12 = f32[1,16,16,64]{3,2,1,0:T(8,128)S(1)} collective-permute-done((f32[1,16,16,64]{3,2,1,0:T(8,128)S(1)}, f32[1,16,16,64]{3,2,1,0:T(8,128)S(1)}, u32[]{:S(2)}, u32[]{:S(2)}) %collective-permute-start.12) | collective-permute-done | bytes 65568 | tf_op jit(solution)/shard_map/ppermute | solution.py:23
  299.7 4.6 %collective-permute-done.18 = f32[16,1,16,64]{3,2,1,0:T(8,128)S(1)} collective-permute-done((f32[16,1,16,64]{3,2,1,0:T(8,128)S(1)}, f32[16,1,16,64]{3,2,1,0:T(8,128)S(1)}, u32[]{:S(2)}, u32[]{:S(2)}) %collective-permute-start.18) | collective-permute-done | bytes 65568 | tf_op jit(solution)/shard_map/ppermute | solution.py:25
  (130 shorter events, 104.9 us)
Async XLA Ops:
  1.4 22.4 %collective-permute-start.7 = (f32[3,16,16]{2,1,0:T(8,128)S(1)}, f32[3,16,16]{2,1,0:T(8,128)S(1)}, u32[]{:S(2)}, u32[]{:S(2)}) collective-permute-start(f32[3,16,16]{2,1,0:T(8,128)S(1)} %get-tuple-element.98), channel_id=1, source_target_pairs={{64,0},{128,64},{192,128},{256,192},{320,256},{384,320},{448,384},... | collective-permute-start | bytes 9224 | tf_op jit(solution)/shard_map/ppermute | solution.py:25
  9.1 13.8 %collective-permute-start.6 = (f32[3,16,16]{2,1,0:T(8,128)S(1)}, f32[3,16,16]{2,1,0:T(8,128)S(1)}, u32[]{:S(2)}, u32[]{:S(2)}) collective-permute-start(f32[3,16,16]{2,1,0:T(8,128)S(1)} %get-tuple-element.99), channel_id=1, source_target_pairs={{0,64},{64,128},{128,192},{192,256},{256,320},{320,384},{384,448},... | collective-permute-start | bytes 9224 | tf_op jit(solution)/shard_map/ppermute | solution.py:23
  12.3 42.7 %collective-permute-start.1 = (f32[3,16,16,64]{3,2,1,0:T(8,128)S(1)}, f32[3,16,16,64]{3,2,1,0:T(8,128)S(1)}, u32[]{:S(2)}, u32[]{:S(2)}) collective-permute-start(f32[3,16,16,64]{3,2,1,0:T(8,128)S(1)} %get-tuple-element.92), channel_id=1, source_target_pairs={{64,0},{128,64},{192,128},{256,192},{320,256},{384,320},{448,384},... | collective-permute-start | bytes 589832 | tf_op jit(solution)/shard_map/ppermute | solution.py:25
  20.9 32.3 %collective-permute-start = (f32[3,16,16,64]{3,2,1,0:T(8,128)S(1)}, f32[3,16,16,64]{3,2,1,0:T(8,128)S(1)}, u32[]{:S(2)}, u32[]{:S(2)}) collective-permute-start(f32[3,16,16,64]{3,2,1,0:T(8,128)S(1)} %get-tuple-element.93), channel_id=1, source_target_pairs={{0,64},{64,128},{128,192},{192,256},{256,320},{320,384},{384,448},... | collective-permute-start | bytes 589832 | tf_op jit(solution)/shard_map/ppermute | solution.py:23
  55.2 21.7 %collective-permute-start.2 = (f32[22,3,16,64]{3,2,1,0:T(8,128)S(1)}, f32[22,3,16,64]{3,2,1,0:T(8,128)S(1)}, u32[]{:S(2)}, u32[]{:S(2)}) collective-permute-start(f32[22,3,16,64]{3,2,1,0:T(8,128)S(1)} %get-tuple-element.84), channel_id=1, source_target_pairs={{0,8},{8,16},{16,24},{24,32},{32,40},{40,48},{48,56},{56,0},{1,9},... | collective-permute-start | bytes 811016 | tf_op jit(solution)/shard_map/ppermute | solution.py:23
  59.5 17.5 %collective-permute-start.3 = (f32[22,3,16,64]{3,2,1,0:T(8,128)S(1)}, f32[22,3,16,64]{3,2,1,0:T(8,128)S(1)}, u32[]{:S(2)}, u32[]{:S(2)}) collective-permute-start(f32[22,3,16,64]{3,2,1,0:T(8,128)S(1)} %get-tuple-element.85), channel_id=1, source_target_pairs={{8,0},{16,8},{24,16},{32,24},{40,32},{48,40},{56,48},{0,56},{9,1},... | collective-permute-start | bytes 811016 | tf_op jit(solution)/shard_map/ppermute | solution.py:25
  68.1 7.2 %collective-permute-start.8 = (f32[22,3,16]{2,1,0:T(4,128)S(1)}, f32[22,3,16]{2,1,0:T(4,128)S(1)}, u32[]{:S(2)}, u32[]{:S(2)}) collective-permute-start(f32[22,3,16]{2,1,0:T(4,128)S(1)} %get-tuple-element.96), channel_id=1, source_target_pairs={{0,8},{8,16},{16,24},{24,32},{32,40},{40,48},{48,56},{56,0},{1,9},... | collective-permute-start | bytes 12680 | tf_op jit(solution)/shard_map/ppermute | solution.py:23
  70.0 6.8 %collective-permute-start.9 = (f32[22,3,16]{2,1,0:T(4,128)S(1)}, f32[22,3,16]{2,1,0:T(4,128)S(1)}, u32[]{:S(2)}, u32[]{:S(2)}) collective-permute-start(f32[22,3,16]{2,1,0:T(4,128)S(1)} %get-tuple-element.97), channel_id=1, source_target_pairs={{8,0},{16,8},{24,16},{32,24},{40,32},{48,40},{56,48},{0,56},{9,1},... | collective-permute-start | bytes 12680 | tf_op jit(solution)/shard_map/ppermute | solution.py:25
  77.5 32.7 %collective-permute-start.5 = (f32[22,22,3,64]{3,1,2,0:T(8,128)S(1)}, f32[22,22,3,64]{3,1,2,0:T(8,128)S(1)}, u32[]{:S(2)}, u32[]{:S(2)}) collective-permute-start(f32[22,22,3,64]{3,1,2,0:T(8,128)S(1)} %copy.20), channel_id=1, source_target_pairs={{1,0},{2,1},{3,2},{4,3},{5,4},{6,5},{7,6},{0,7},{9,8},{10,9},{11,1... | collective-permute-start | bytes 1115144 | tf_op jit(solution)/shard_map/ppermute | solution.py:25
  79.5 31.0 %collective-permute-start.4 = (f32[22,22,3,64]{3,1,2,0:T(8,128)S(1)}, f32[22,22,3,64]{3,1,2,0:T(8,128)S(1)}, u32[]{:S(2)}, u32[]{:S(2)}) collective-permute-start(f32[22,22,3,64]{3,1,2,0:T(8,128)S(1)} %copy.19), channel_id=1, source_target_pairs={{0,1},{1,2},{2,3},{3,4},{4,5},{5,6},{6,7},{7,0},{8,9},{9,10},{10,1... | collective-permute-start | bytes 1115144 | tf_op jit(solution)/shard_map/ppermute | solution.py:23
  82.0 27.1 %collective-permute-start.10 = (f32[22,22,3]{2,1,0:T(8,128)S(1)}, f32[22,22,3]{2,1,0:T(8,128)S(1)}, u32[]{:S(2)}, u32[]{:S(2)}) collective-permute-start(f32[22,22,3]{2,1,0:T(8,128)S(1)} %get-tuple-element.94), channel_id=1, source_target_pairs={{0,1},{1,2},{2,3},{3,4},{4,5},{5,6},{6,7},{7,0},{8,9},{9,10},{10,1... | collective-permute-start | bytes 17432 | tf_op jit(solution)/shard_map/ppermute | solution.py:23
  90.3 18.8 %collective-permute-start.11 = (f32[22,22,3]{2,1,0:T(8,128)S(1)}, f32[22,22,3]{2,1,0:T(8,128)S(1)}, u32[]{:S(2)}, u32[]{:S(2)}) collective-permute-start(f32[22,22,3]{2,1,0:T(8,128)S(1)} %get-tuple-element.95), channel_id=1, source_target_pairs={{1,0},{2,1},{3,2},{4,3},{5,4},{6,5},{7,6},{0,7},{9,8},{10,9},{11,1... | collective-permute-start | bytes 17432 | tf_op jit(solution)/shard_map/ppermute | solution.py:25
  185.8 121.2 %collective-permute-start.20 = (f32[16,16,1,64]{3,2,1,0:T(1,128)S(1)}, f32[16,16,1,64]{3,2,1,0:T(1,128)S(1)}, u32[]{:S(2)}, u32[]{:S(2)}) collective-permute-start(f32[16,16,1,64]{3,2,1,0:T(1,128)S(1)} %get-tuple-element.81), channel_id=1, source_target_pairs={{0,1},{1,2},{2,3},{3,4},{4,5},{5,6},{6,7},{7,0},{8,9},{9,10},{10,1... | collective-permute-start | bytes 196616 | tf_op jit(solution)/shard_map/ppermute | solution.py:23
  188.9 117.7 %collective-permute-start.22 = (f32[16,16,1,64]{3,2,1,0:T(1,128)S(1)}, f32[16,16,1,64]{3,2,1,0:T(1,128)S(1)}, u32[]{:S(2)}, u32[]{:S(2)}) collective-permute-start(f32[16,16,1,64]{3,2,1,0:T(1,128)S(1)} %get-tuple-element.80), channel_id=1, source_target_pairs={{1,0},{2,1},{3,2},{4,3},{5,4},{6,5},{7,6},{0,7},{9,8},{10,9},{11,1... | collective-permute-start | bytes 196616 | tf_op jit(solution)/shard_map/ppermute | solution.py:25
  196.3 111.5 %collective-permute-start.21 = (f32[16,16,1,64]{3,2,1,0:T(1,128)S(1)}, f32[16,16,1,64]{3,2,1,0:T(1,128)S(1)}, u32[]{:S(2)}, u32[]{:S(2)}) collective-permute-start(f32[16,16,1,64]{3,2,1,0:T(1,128)S(1)} %get-tuple-element.91), channel_id=1, source_target_pairs={{0,1},{1,2},{2,3},{3,4},{4,5},{5,6},{6,7},{7,0},{8,9},{9,10},{10,1... | collective-permute-start | bytes 196616 | tf_op jit(solution)/shard_map/ppermute | solution.py:23
  198.6 108.8 %collective-permute-start.23 = (f32[16,16,1,64]{3,2,1,0:T(1,128)S(1)}, f32[16,16,1,64]{3,2,1,0:T(1,128)S(1)}, u32[]{:S(2)}, u32[]{:S(2)}) collective-permute-start(f32[16,16,1,64]{3,2,1,0:T(1,128)S(1)} %get-tuple-element.90), channel_id=1, source_target_pairs={{1,0},{2,1},{3,2},{4,3},{5,4},{6,5},{7,6},{0,7},{9,8},{10,9},{11,1... | collective-permute-start | bytes 196616 | tf_op jit(solution)/shard_map/ppermute | solution.py:25
  212.4 24.3 %collective-permute-start.19 = (f32[16,1,16,64]{3,1,2,0:T(1,128)S(1)}, f32[16,1,16,64]{3,1,2,0:T(1,128)S(1)}, u32[]{:S(2)}, u32[]{:S(2)}) collective-permute-start(f32[16,1,16,64]{3,1,2,0:T(1,128)S(1)} %get-tuple-element.88), channel_id=1, source_target_pairs={{8,0},{16,8},{24,16},{32,24},{40,32},{48,40},{56,48},{0,56},{9,1},... | collective-permute-start | bytes 196616 | tf_op jit(solution)/shard_map/ppermute | solution.py:25
  236.7 8.1 %collective-permute-start.17 = (f32[16,1,16,64]{3,1,2,0:T(1,128)S(1)}, f32[16,1,16,64]{3,1,2,0:T(1,128)S(1)}, u32[]{:S(2)}, u32[]{:S(2)}) collective-permute-start(f32[16,1,16,64]{3,1,2,0:T(1,128)S(1)} %get-tuple-element.89), channel_id=1, source_target_pairs={{0,8},{8,16},{16,24},{24,32},{32,40},{40,48},{48,56},{56,0},{1,9},... | collective-permute-start | bytes 196616 | tf_op jit(solution)/shard_map/ppermute | solution.py:23
  244.8 14.3 %collective-permute-start.15 = (f32[1,16,16,64]{3,0,2,1:T(1,128)S(1)}, f32[1,16,16,64]{3,0,2,1:T(1,128)S(1)}, u32[]{:S(2)}, u32[]{:S(2)}) collective-permute-start(f32[1,16,16,64]{3,0,2,1:T(1,128)S(1)} %get-tuple-element.86), channel_id=1, source_target_pairs={{64,0},{128,64},{192,128},{256,192},{320,256},{384,320},{448,384},... | collective-permute-start | bytes 196616 | tf_op jit(solution)/shard_map/ppermute | solution.py:25
  259.1 13.0 %collective-permute-start.13 = (f32[1,16,16,64]{3,0,2,1:T(1,128)S(1)}, f32[1,16,16,64]{3,0,2,1:T(1,128)S(1)}, u32[]{:S(2)}, u32[]{:S(2)}) collective-permute-start(f32[1,16,16,64]{3,0,2,1:T(1,128)S(1)} %get-tuple-element.87), channel_id=1, source_target_pairs={{0,64},{64,128},{128,192},{192,256},{256,320},{320,384},{384,448},... | collective-permute-start | bytes 196616 | tf_op jit(solution)/shard_map/ppermute | solution.py:23
  272.1 13.6 %collective-permute-start.14 = (f32[1,16,16,64]{3,2,1,0:T(8,128)S(1)}, f32[1,16,16,64]{3,2,1,0:T(8,128)S(1)}, u32[]{:S(2)}, u32[]{:S(2)}) collective-permute-start(f32[1,16,16,64]{3,2,1,0:T(8,128)S(1)} %get-tuple-element.78), channel_id=1, source_target_pairs={{64,0},{128,64},{192,128},{256,192},{320,256},{384,320},{448,384},... | collective-permute-start | bytes 196616 | tf_op jit(solution)/shard_map/ppermute | solution.py:25
  285.7 11.7 %collective-permute-start.12 = (f32[1,16,16,64]{3,2,1,0:T(8,128)S(1)}, f32[1,16,16,64]{3,2,1,0:T(8,128)S(1)}, u32[]{:S(2)}, u32[]{:S(2)}) collective-permute-start(f32[1,16,16,64]{3,2,1,0:T(8,128)S(1)} %get-tuple-element.79), channel_id=1, source_target_pairs={{0,64},{64,128},{128,192},{192,256},{256,320},{320,384},{384,448},... | collective-permute-start | bytes 196616 | tf_op jit(solution)/shard_map/ppermute | solution.py:23
  297.4 6.8 %collective-permute-start.18 = (f32[16,1,16,64]{3,2,1,0:T(8,128)S(1)}, f32[16,1,16,64]{3,2,1,0:T(8,128)S(1)}, u32[]{:S(2)}, u32[]{:S(2)}) collective-permute-start(f32[16,1,16,64]{3,2,1,0:T(8,128)S(1)} %get-tuple-element.76), channel_id=1, source_target_pairs={{8,0},{16,8},{24,16},{32,24},{40,32},{48,40},{56,48},{0,56},{9,1},... | collective-permute-start | bytes 196616 | tf_op jit(solution)/shard_map/ppermute | solution.py:25
  304.3 8.1 %collective-permute-start.16 = (f32[16,1,16,64]{3,2,1,0:T(8,128)S(1)}, f32[16,1,16,64]{3,2,1,0:T(8,128)S(1)}, u32[]{:S(2)}, u32[]{:S(2)}) collective-permute-start(f32[16,1,16,64]{3,2,1,0:T(8,128)S(1)} %get-tuple-element.77), channel_id=1, source_target_pairs={{0,8},{8,16},{16,24},{24,32},{32,40},{40,48},{48,56},{56,0},{1,9},... | collective-permute-start | bytes 196616 | tf_op jit(solution)/shard_map/ppermute | solution.py:23
  (12 other events, 160.9 us)
where the time goes:
time: 320 us; the launch traced here: 316 us
  starting transfers between devices  103 us (32%)
  waiting for transfers between devices  91.7 us (29%)
  matrix products  82.9 us (26%)
  local copies, waits for them, and re-layouts  31.5 us (10%)
  other arithmetic  5 us (2%)
    ppermute x12, waiting for transfers between devices, extended(): lax.ppermute(tail, axis, [(i, (i + 1) % count) for i in range(count)])  75.3 us
    ppermute x12, starting transfers between devices, extended(): lax.ppermute(head, axis, [((i + 1) % count, i) for i in range(count)])  68.8 us
    dot_general x5, matrix products, apply_along(): jnp.einsum(forms[axis_pos], matrix, field, precision=lax.Precision.HIGHEST)  40.2 us
    ppermute x12, starting transfers between devices, extended(): lax.ppermute(tail, axis, [(i, (i + 1) % count) for i in range(count)])  34.3 us
    ppermute x12, waiting for transfers between devices, extended(): lax.ppermute(head, axis, [((i + 1) % count, i) for i in range(count)])  16.4 us
    dot_general x36, matrix products, face_product(): jnp.einsum('...pqi,...pqj->...ij', left, right, precision=lax.Precision.H...  13.7 us
    reshape x2, local copies, waits for them, and re-layouts, hamiltonian(): (along_x + along_y).reshape(field.shape) + apply_along(deriv_two, field, 2)  11.2 us
    dot_general x3, matrix products, assemble(): jnp.einsum(volume_form, gradients[axis_pos], gradients[axis_pos], precisi...  10.9 us
  transfers between devices with their start and end apart: 24, of which 11 were waited for; matrix products, arithmetic and copies ran while one was open for 13% of the time, Pallas kernels for 0%

commit v1 on v0

v1 whole, which is shorter than its diff:
```python
import functools

import jax
import jax.numpy as jnp
import numpy as np
from jax import lax
from jax.experimental import pallas as pl
from jax.experimental.pallas import tpu as pltpu
from jax.sharding import PartitionSpec as P

BUF = 3
CELLS = 16
EXT = 22
ORB = 64
HALF = EXT // 2
PENALTY = 2.0
LOW_BOUND = -1.5
CUTOFF = 8.0
HIGH_BOUND = 16.0

YLO, YHI, ZLO, ZHI, ROWS = 256, 304, 352, 424, 496
ZPAD = 24
MESSAGE = 392
AXES = ("gx", "gy", "gz")
MESH = pl.DeviceIdType.MESH
F32 = jnp.float32
BF16 = jnp.bfloat16


def spectral_tables(points):
    indices = np.arange(points)
    offsets = indices[:, None] - indices[None, :]
    nyquist = points // 2
    deriv_one = np.zeros((points, points))
    deriv_two = np.zeros((points, points))
    for harmonic in range(1, nyquist):
        wavenum = 2.0 * np.pi * harmonic / points
        deriv_one = deriv_one - 2.0 * wavenum * np.sin(wavenum * offsets) / points
        deriv_two = deriv_two - 2.0 * wavenum * wavenum * np.cos(wavenum * offsets) / points
    deriv_two = deriv_two - np.pi * np.pi * np.cos(np.pi * offsets) / points
    return deriv_one, deriv_two


def row_cells():
    cells = [(-1, -1)] * ROWS
    for y in range(CELLS):
        for z in range(CELLS):
            cells[y * CELLS + z] = (BUF + y, BUF + z)
    for h in range(BUF):
        for z in range(CELLS):
            cells[YLO + h * CELLS + z] = (h, BUF + z)
            cells[YHI + h * CELLS + z] = (BUF + CELLS + h, BUF + z)
        for k in range(EXT):
            y = BUF + k if k < CELLS else (k - CELLS if k < CELLS + BUF else k)
            cells[ZLO + h * ZPAD + k] = (y, h)
            cells[ZHI + h * ZPAD + k] = (y, BUF + CELLS + h)
    return np.array(cells)


def split_host(matrix):
    full = jnp.asarray(matrix, F32)
    high = full.astype(BF16)
    low = (full - high.astype(F32)).astype(BF16)
    return jnp.concatenate([high, low, high], axis=1)


def plane_matrices():
    deriv_one, deriv_two = spectral_tables(EXT)
    cells = row_cells()
    real = (cells[:, 0] >= 0).astype(np.float64)
    ys, zs = np.maximum(cells[:, 0], 0), np.maximum(cells[:, 1], 0)
    same_y = (ys[:, None] == ys[None, :]) * real[:, None] * real[None, :]
    same_z = (zs[:, None] == zs[None, :]) * real[:, None] * real[None, :]
    kinetic = -0.5 * (same_z * deriv_two[ys[:, None], ys[None, :]] + same_y * deriv_two[zs[:, None], zs[None, :]])
    grad_y = (same_z * deriv_one[ys[:, None], ys[None, :]])[:YLO]
    grad_z = (same_y * deriv_one[zs[:, None], zs[None, :]])[:YLO]
    return split_host(kinetic), split_host(np.concatenate([grad_y, grad_z], axis=0))


def pair_coefs():
    deriv_one, deriv_two = spectral_tables(EXT)
    second = np.zeros((16, 128))
    first = np.zeros((16, 128))
    for d in range(HALF):
        for table, out, factor in ((deriv_two, second, -0.25), (deriv_one, first, 0.5)):
            near, far = table[d, 0], table[(d + HALF) % EXT, 0]
            out[d, :ORB] = factor * (near + far)
            out[d, ORB:] = factor * (near - far)
    return jnp.asarray(np.concatenate([second, first]), F32)


def cheb_constants():
    half_width = (HIGH_BOUND - CUTOFF) / 2.0
    center = (HIGH_BOUND + CUTOFF) / 2.0
    scale_now = half_width / (LOW_BOUND - center)
    scale_next = 1.0 / (2.0 / scale_now - scale_now)
    return center, scale_now / half_width, 2.0 * scale_next / half_width, scale_now * scale_next


def split(value):
    high = value.astype(BF16)
    return high, (value - high.astype(F32)).astype(BF16)


def stacked(value):
    high, low = split(value)
    return jnp.concatenate([high, high, low], axis=0)


def swap(value):
    return pltpu.roll(value, ORB, 1)


def matmul(left, right):
    return jnp.dot(left, right, preferred_element_type=F32)


def gram(left, right):
    return lax.dot_general(left, right, (((0,), (0,)), ((), ())), preferred_element_type=F32)


def gram_split(left, right):
    (lh, ll), (rh, rl) = left, right
    return gram(lh, rh) + (gram(lh, rl) + gram(ll, rh))


def left_lanes(rows):
    return lax.broadcasted_iota(jnp.int32, (rows, 128), 1) < ORB


def kernel(
    x_ref, pot_ref, kin_ref, grad_ref, coef_ref,
    basis_ref, blocks_ref,
    xs, xr, pot_s, cells, pots, work, filt, zs, gx, gyz, faces, others,
    xsend, xrecv, ysend, yrecv, zsend, zrecv, fsend, frecv,
):
    center, alpha, beta, gamma = cheb_constants()
    me = [lax.axis_index(a) for a in AXES]
    size = [lax.axis_size(a) for a in AXES]

    def beside(axis, step):
        return {AXES[axis]: lax.rem(me[axis] + step + size[axis], size[axis])}

    barrier = pltpu.get_barrier_semaphore()
    for axis in range(3):
        for step in (-1, 1):
            pl.semaphore_signal(barrier, inc=1, device_id=beside(axis, step), device_id_type=MESH)

    def send(src, dst, ssem, rsem, axis, step):
        copy = pltpu.make_async_remote_copy(
            src_ref=src, dst_ref=dst, send_sem=ssem, recv_sem=rsem,
            device_id=beside(axis, step), device_id_type=MESH,
        )
        copy.start()
        return copy

    for side, start in ((0, 0), (1, CELLS - BUF)):
        for j in range(BUF):
            xs[side, j * 128 : (j + 1) * 128, :] = jnp.concatenate(
                [x_ref[start + j, :8].reshape(128, ORB), x_ref[start + j, 8:].reshape(128, ORB)], axis=1
            )
    xs[0, 384:392, :] = pot_ref[0:8, :]
    xs[1, 384:392, :] = pot_ref[24:32, :]
    zs[...] = jnp.zeros_like(zs)
    pl.semaphore_wait(barrier, 6)
    xcopies = [
        send(xs.at[0], xr.at[0], xsend.at[0], xrecv.at[0], 0, -1),
        send(xs.at[1], xr.at[1], xsend.at[1], xrecv.at[1], 0, 1),
    ]

    zero = jnp.zeros((256, ORB), F32)
    for a in range(HALF):
        low = x_ref[a - BUF].reshape(256, ORB) if a >= BUF else zero
        high = x_ref[a + 8].reshape(256, ORB) if a < 8 else zero
        cells[a, :256, :] = jnp.concatenate([low, high], axis=1)
    for copy in xcopies:
        copy.wait()
    keep = left_lanes(128)
    for j in range(BUF):
        got = xr[1, j * 128 : (j + 1) * 128, :]
        cells[j, 0:128, :] = jnp.where(keep, got, cells[j, 0:128, :])
        cells[j, 128:256, :] = jnp.where(keep, swap(got), cells[j, 128:256, :])
        got = xr[0, j * 128 : (j + 1) * 128, :]
        cells[8 + j, 0:128, :] = jnp.where(keep, cells[8 + j, 0:128, :], swap(got))
        cells[8 + j, 128:256, :] = jnp.where(keep, cells[8 + j, 128:256, :], got)
    pot_s[0:6, :] = xr[1, 386:392, :]
    pot_s[6:38, :] = pot_ref[...]
    pot_s[38:44, :] = xr[0, 384:390, :]
    pot_s[44:48, :] = jnp.zeros((4, 128), F32)
    for h in range(2):
        part = jnp.concatenate([pot_s[pl.ds(h, 24, stride=2), :], jnp.zeros((104, 128), F32)], axis=0)
        cells[HALF, h * 128 : (h + 1) * 128, :] = part.T

    ycopies = [
        send(cells.at[:, 0:48, :], cells.at[:, YHI : YHI + 48, :], ysend.at[0], yrecv.at[0], 1, -1),
        send(cells.at[:, 208:256, :], cells.at[:, YLO : YLO + 48, :], ysend.at[1], yrecv.at[1], 1, 1),
    ]
    for copy in ycopies:
        copy.wait()

    @pl.loop(0, HALF + 1)
    def _(a):
        for side, start in ((0, 0), (1, CELLS - BUF)):
            for h in range(BUF):
                zs[side, a, h * ZPAD : h * ZPAD + EXT, :] = cells[a, pl.ds(start + h, EXT, stride=CELLS), :]

    zcopies = [
        send(zs.at[0], cells.at[:, ZHI : ZHI + 72, :], zsend.at[0], zrecv.at[0], 2, -1),
        send(zs.at[1], cells.at[:, ZLO : ZLO + 72, :], zsend.at[1], zrecv.at[1], 2, 1),
    ]
    for copy in zcopies:
        copy.wait()

    sign = jnp.where(left_lanes(8), 1.0, -1.0).astype(F32)

    def along_x(planes, base, odd, out):
        coefs = [jnp.broadcast_to(coef_ref[base + d : base + d + 1, :], (8, 128)) for d in range(HALF)]
        mixed = [swap(v) + sign * v for v in planes]
        for a in range(HALF):
            total = None
            for b in range(HALF):
                if odd and a == b:
                    continue
                term = coefs[abs(a - b)] * mixed[b]
                if total is None:
                    total = term if not (odd and a < b) else -term
                else:
                    total = total - term if odd and a < b else total + term
            out(a, swap(total) + sign * total)

    @pl.loop(0, ROWS // 8)
    def _(r):
        rows = pl.ds(pl.multiple_of(r * 8, 8), 8)
        planes = [cells[a, rows, :] for a in range(HALF)]
        column = cells[HALF, rows, :]
        keep8 = left_lanes(8)

        def out(a, value):
            pot = jnp.where(
                keep8,
                jnp.broadcast_to(column[:, a : a + 1], (8, 128)),
                jnp.broadcast_to(column[:, a + HALF : a + HALF + 1], (8, 128)),
            )
            pots[a, rows, :] = pot
            work[a, rows, :] = value + (pot - center) * planes[a]

        along_x(planes, 0, False, out)

    work[HALF] = jnp.zeros((ROWS, 128), F32)

    @pl.loop(0, 6)
    def _(g):
        pair = jnp.concatenate([cells[2 * g], cells[2 * g + 1]], axis=1)
        done = matmul(kin_ref[...], stacked(pair))
        work[2 * g] = work[2 * g] + done[:, :128]
        work[2 * g + 1] = work[2 * g + 1] + done[:, 128:]

    @pl.loop(0, ROWS // 8)
    def _(r):
        rows = pl.ds(pl.multiple_of(r * 8, 8), 8)
        planes = [work[a, rows, :] for a in range(HALF)]

        def out(a, value):
            applied = value + (pots[a, rows, :] - center) * planes[a]
            filt[a, rows, :] = (alpha * beta) * applied - gamma * cells[a, rows, :]

        along_x(planes, 0, False, out)

    filt[HALF] = jnp.zeros((ROWS, 128), F32)

    @pl.loop(0, 6)
    def _(g):
        pair = jnp.concatenate([work[2 * g], work[2 * g + 1]], axis=1)
        done = (alpha * beta) * matmul(kin_ref[...], stacked(pair))
        filt[2 * g] = filt[2 * g] + done[:, :128]
        filt[2 * g + 1] = filt[2 * g + 1] + done[:, 128:]

    @pl.loop(0, 32)
    def _(r):
        rows = pl.ds(pl.multiple_of(r * 8, 8), 8)
        planes = [filt[a, rows, :] for a in range(HALF)]

        def out(a, value):
            gx[a, rows, :] = value

        along_x(planes, 16, True, out)

    keep256 = left_lanes(256)
    faces[0] = jnp.where(keep256, filt[3, :256, :], swap(gx[3]))
    faces[1] = jnp.where(keep256, swap(filt[7, :256, :]), gx[7])
    fcopies = [
        send(faces.at[0], others.at[1], fsend.at[0], frecv.at[1], 0, -1),
        send(faces.at[1], others.at[0], fsend.at[1], frecv.at[0], 0, 1),
    ]

    @pl.loop(0, 6)
    def _(g):
        pair = jnp.concatenate([filt[2 * g], filt[2 * g + 1]], axis=1)
        done = matmul(grad_ref[...], stacked(pair))
        gyz[2 * g] = done[:, :128]
        gyz[2 * g + 1] = done[:, 128:]

    keep16 = left_lanes(16)
    for i in range(CELLS):
        a, lower = (i + BUF, True) if i < 8 else (i - 8, False)
        for side, layer in ((0, 0), (1, CELLS - 1)):
            value = filt[a, layer * 16 : layer * 16 + 16, :]
            deriv = gyz[a, layer * 16 : layer * 16 + 16, :]
            faces[2 + side, i * 16 : i * 16 + 16, :] = (
                jnp.where(keep16, value, swap(deriv)) if lower else jnp.where(keep16, swap(value), deriv)
            )
            value = filt[a, pl.ds(layer, 16, stride=16), :]
            deriv = gyz[a, pl.ds(256 + layer, 16, stride=16), :]
            faces[4 + side, i * 16 : i * 16 + 16, :] = (
                jnp.where(keep16, value, swap(deriv)) if lower else jnp.where(keep16, swap(value), deriv)
            )
    for axis in (1, 2):
        fcopies.append(send(faces.at[2 * axis], others.at[2 * axis + 1], fsend.at[2 * axis], frecv.at[2 * axis + 1], axis, -1))
        fcopies.append(send(faces.at[2 * axis + 1], others.at[2 * axis], fsend.at[2 * axis + 1], frecv.at[2 * axis], axis, 1))

    for i in range(CELLS):
        a, lower = (i + BUF, True) if i < 8 else (i - 8, False)
        value = filt[a, :256, :]
        value = value[:, :ORB] if lower else swap(value)[:, :ORB]
        basis_ref[i] = value.reshape(16, 16, ORB)

    def volume(a, total):
        inside = jnp.where(keep256, (a >= BUF).astype(F32), (a < 8).astype(F32))
        value = filt[a, :256, :]
        mass = gram_split(split(value), split(inside * pots[a, :256, :] * value))
        square = jnp.zeros((128, 128), F32)
        for part in (gx[a], gyz[a, :256, :], gyz[a, 256:, :]):
            high, low = split(inside * part)
            square = square + (gram(high, high) + gram(high, low) + gram(low, high))
        return total + mass + 0.5 * square

    total = lax.fori_loop(0, HALF, volume, jnp.zeros((128, 128), F32))
    diagonal = total[:ORB, :ORB] + total[ORB:, ORB:]
    for f in range(6):
        s = -1.0 if f % 2 == 0 else 1.0
        pair = split(faces[f])
        own = gram_split(pair, pair)
        diagonal = diagonal - (0.25 * s) * (own[:ORB, ORB:] + own[ORB:, :ORB]) + (0.5 * PENALTY) * own[:ORB, :ORB]
    blocks_ref[0] = diagonal
    for f in (2, 3, 4, 5, 0, 1):
        fcopies[f ^ 1].wait_recv()
        s = -1.0 if f % 2 == 0 else 1.0
        both = gram_split(split(faces[f]), split(others[f]))
        blocks_ref[1 + f] = (0.25 * s) * (both[ORB:, :ORB] - both[:ORB, ORB:]) - (0.5 * PENALTY) * both[:ORB, :ORB]
    for copy in fcopies:
        copy.wait_send()


def on_device(orbitals, potential):
    kinetic, gradient = plane_matrices()
    vmem = pl.BlockSpec(memory_space=pltpu.VMEM)
    dma = pltpu.SemaphoreType.DMA
    basis, blocks = pl.pallas_call(
        kernel,
        out_shape=(
            jax.ShapeDtypeStruct((CELLS, CELLS, CELLS, ORB), F32),
            jax.ShapeDtypeStruct((7, ORB, ORB), F32),
        ),
        in_specs=[vmem] * 5,
        out_specs=(vmem, vmem),
        scratch_shapes=[
            pltpu.VMEM((2, MESSAGE, 128), F32),
            pltpu.VMEM((2, MESSAGE, 128), F32),
            pltpu.VMEM((48, 128), F32),
            pltpu.VMEM((12, ROWS, 128), F32),
            pltpu.VMEM((HALF, ROWS, 128), F32),
            pltpu.VMEM((12, ROWS, 128), F32),
            pltpu.VMEM((12, ROWS, 128), F32),
            pltpu.VMEM((2, 12, 72, 128), F32),
            pltpu.VMEM((HALF, 256, 128), F32),
            pltpu.VMEM((12, 512, 128), F32),
            pltpu.VMEM((6, 256, 128), F32),
            pltpu.VMEM((6, 256, 128), F32),
            dma((2,)), dma((2,)), dma((2,)), dma((2,)), dma((2,)), dma((2,)), dma((6,)), dma((6,)),
        ],
        compiler_params=pltpu.CompilerParams(
            collective_id=0, has_side_effects=True, vmem_limit_bytes=60 * 1024 * 1024
        ),
    )(orbitals, potential.reshape(32, 128), kinetic, gradient, pair_coefs())
    return basis, blocks[None, None, None]


def solution(mesh):
    return jax.shard_map(
        on_device,
        mesh=mesh,
        in_specs=(P("gx", "gy", "gz", None), P("gx", "gy", "gz")),
        out_specs=(P("gx", "gy", "gz", None), P("gx", "gy", "gz", None, None, None)),
        check_vma=False,
    )
```

time: 320 us -> 115 us (0.36)
  the two profiles are of different devices: /device:TPU:2 before, /device:TPU:17 now
where the time goes in v1:
time: 115 us
  Pallas kernels  108 us (94%)
  local copies, waits for them, and re-layouts  5.44 us (5%)
    pallas_call x1, Pallas kernels, on_device(): pl.pallas_call(kernel, out_shape=(jax.ShapeDtypeStruct((CELLS, CELLS, CEL...  108 us
    unnamed x4, local copies, waits for them, and re-layouts  3.83 us

profile of v1, /device:TPU:17, one launch (start us, length us, event | category | flops | bytes accessed | tf_op | source)
XLA Modules:
  0.0 114.5 jit_solution(8467784299988406599)
XLA Ops:
  0.6 1.6 %reshape.7.pot_ref = f32[32,128]{1,0:T(8,128)} reshape(f32[16,16,16]{2,1,0:T(8,128)} %param.6) | data formatting | bytes 32768 | tf_op jit(solution)/shard_map/reshape | solution.py:384
  2.2 108.5 %shard_map.68 = (f32[16,16,16,64]{3,2,1,0:T(8,128)}, f32[7,64,64]{2,1,0:T(8,128)}) custom-call(f32[16,16,16,64]{3,2,1,0:T(8,128)} %x_ref.1, f32[32,128]{1,0:T(8,128)} %reshape.7.pot_ref, bf16[496,1488]{1,0:T(8,128)(2,1)} %constant.13.kin_ref, bf16[512,1488]{1,0:T(8,128)(2,1)} %constant.18.grad_ref, f32[32,128]{1,0:T(8,128)} %constant.8.clone.coef_ref), custom_call_target="tpu_custom_call" | custom-call | tf_op jit(solution)/shard_map/pallas_call | solution.py:358
  110.7 0.0 copy-start
  110.7 3.1 %copy.9 = f32[16,16,16,64]{3,2,1,0:T(8,128)} copy(f32[16,16,16,64]{3,2,1,0:T(8,128)} %get-tuple-element.8) | data formatting | bytes 2097152
  113.8 0.0 copy-done
  113.9 0.7 copy.10
Async XLA Ops:
  110.7 3.1 %copy-start = (f32[7,64,64]{2,1,0:T(8,128)S(1)}, f32[7,64,64]{2,1,0:T(8,128)}, u32[]{:S(2)}) copy-start(f32[7,64,64]{2,1,0:T(8,128)} %get-tuple-element.5) | copy-start | bytes 344068

commit v2 on v1

v2 whole, which is shorter than its diff:
```python
import functools

import jax
import jax.numpy as jnp
import numpy as np
from jax import lax
from jax.experimental import pallas as pl
from jax.experimental.pallas import tpu as pltpu
from jax.sharding import PartitionSpec as P

BUF = 3
CELLS = 16
EXT = 22
ORB = 64
HALF = EXT // 2
OWN = CELLS // 2
PENALTY = 2.0
LOW_BOUND = -1.5
CUTOFF = 8.0
HIGH_BOUND = 16.0

YLO, YHI, ZLO, ZHI, CLO, CHI, ROWS = 256, 304, 352, 400, 448, 472, 496
INNER = 256
CROSS = 448
HALO, POT, PLANES = 8, 11, 12
CHUNKS = ((0, 128), (128, 128), (256, 136))
MESSAGE = 392
AXES = ("gx", "gy", "gz")
MESH = pl.DeviceIdType.MESH
F32 = jnp.float32
BF16 = jnp.bfloat16


def spectral_tables(points):
    indices = np.arange(points)
    offsets = indices[:, None] - indices[None, :]
    nyquist = points // 2
    deriv_one = np.zeros((points, points))
    deriv_two = np.zeros((points, points))
    for harmonic in range(1, nyquist):
        wavenum = 2.0 * np.pi * harmonic / points
        deriv_one = deriv_one - 2.0 * wavenum * np.sin(wavenum * offsets) / points
        deriv_two = deriv_two - 2.0 * wavenum * wavenum * np.cos(wavenum * offsets) / points
    deriv_two = deriv_two - np.pi * np.pi * np.cos(np.pi * offsets) / points
    return deriv_one, deriv_two


def row_cells():
    cells = [(-1, -1)] * ROWS
    for y in range(CELLS):
        for z in range(CELLS):
            cells[y * CELLS + z] = (BUF + y, BUF + z)
    for h in range(BUF):
        for k in range(CELLS):
            cells[YLO + h * CELLS + k] = (h, BUF + k)
            cells[YHI + h * CELLS + k] = (BUF + CELLS + h, BUF + k)
            cells[ZLO + h * CELLS + k] = (BUF + k, h)
            cells[ZHI + h * CELLS + k] = (BUF + k, BUF + CELLS + h)
        for k in range(2 * BUF):
            z = k if k < BUF else CELLS + k
            cells[CLO + h * 8 + k] = (h, z)
            cells[CHI + h * 8 + k] = (BUF + CELLS + h, z)
    return np.array(cells)


def split_host(matrix):
    full = jnp.asarray(matrix, F32)
    high = full.astype(BF16)
    low = (full - high.astype(F32)).astype(BF16)
    parts = [jnp.concatenate([m[:, k] for m in (high, low, high)], axis=1) for k in (slice(0, INNER), slice(INNER, None))]
    return jnp.concatenate(parts, axis=1)


def plane_matrices():
    deriv_one, deriv_two = spectral_tables(EXT)
    cells = row_cells()
    real = (cells[:, 0] >= 0).astype(np.float64)
    ys, zs = np.maximum(cells[:, 0], 0), np.maximum(cells[:, 1], 0)
    same_y = (ys[:, None] == ys[None, :]) * real[:, None] * real[None, :]
    same_z = (zs[:, None] == zs[None, :]) * real[:, None] * real[None, :]
    kinetic = -0.5 * (same_z * deriv_two[ys[:, None], ys[None, :]] + same_y * deriv_two[zs[:, None], zs[None, :]])
    grad_y = (same_z * deriv_one[ys[:, None], ys[None, :]])[:INNER, :CROSS]
    grad_z = (same_y * deriv_one[zs[:, None], zs[None, :]])[:INNER, :CROSS]
    return split_host(kinetic), split_host(np.concatenate([grad_y, grad_z], axis=0))


def pair_tables():
    deriv_one, deriv_two = spectral_tables(EXT)
    lanes = np.arange(128) < ORB

    def entry(table, factor, d):
        near, far = table[d % EXT, 0], table[(d + HALF) % EXT, 0]
        return factor * np.where(lanes, near + far, near - far)

    second, first = [], []
    two = lambda d: entry(deriv_two, -0.25, d)
    one = lambda d: entry(deriv_one, 0.5, d)
    keys_two, keys_one = {}, {}

    def put(keys, rows, key, value):
        keys[key] = len(rows)
        rows.append(value)

    for a in range(5):
        for b in range(a, 5):
            put(keys_two, second, ("e", a, b), 0.5 * (two(a - b) + two(10 - a - b)))
            put(keys_two, second, ("o", a, b), 0.5 * (two(a - b) - two(10 - a - b)))
    for d in range(6):
        put(keys_two, second, ("m", d), two(d))
    for a in range(5):
        for b in range(5):
            put(keys_one, first, ("q", a, b), 0.5 * (one(a - b) - one(a + b - 10)))
    for d in range(1, 6):
        put(keys_one, first, ("m", d), one(d))
    return np.array(second), keys_two, np.array(first), keys_one


SECOND, KEYS_TWO, FIRST, KEYS_ONE = pair_tables()


def cheb_constants():
    half_width = (HIGH_BOUND - CUTOFF) / 2.0
    center = (HIGH_BOUND + CUTOFF) / 2.0
    scale_now = half_width / (LOW_BOUND - center)
    scale_next = 1.0 / (2.0 / scale_now - scale_now)
    return center, scale_now / half_width, 2.0 * scale_next / half_width, scale_now * scale_next


def split(value):
    high = value.astype(BF16)
    return high, (value - high.astype(F32)).astype(BF16)


def stacked(value):
    high, low = split(value)
    return jnp.concatenate([high, high, low], axis=0)


def both_stacked(value):
    return jnp.concatenate([stacked(value[:INNER]), stacked(value[INNER:])], axis=0)


def swap(value):
    return pltpu.roll(value, ORB, 1)


def matmul(left, right):
    return jnp.dot(left, right, preferred_element_type=F32)


def gram(left, right):
    return lax.dot_general(left, right, (((0,), (0,)), ((), ())), preferred_element_type=F32)


def gram_split(left, right):
    (lh, ll), (rh, rl) = left, right
    return gram(lh, rh) + (gram(lh, rl) + gram(ll, rh))


def left_lanes(rows):
    return lax.broadcasted_iota(jnp.int32, (rows, 128), 1) < ORB


def kernel(
    x_hbm, pot_ref, kin_hbm, grad_hbm, two_ref, one_ref,
    basis_ref, blocks_ref,
    x_ref, kin_ref, grad_ref, spread_ref,
    xs, xr, flat, pot_s, cells, pots, work, filt, zs, cs, gx, gyz, faces, others,
    local, xsend, xrecv, ysend, yrecv, zsend, zrecv, csend, crecv, fsend, frecv,
):
    center, alpha, beta, gamma = cheb_constants()
    me = [lax.axis_index(a) for a in AXES]
    size = [lax.axis_size(a) for a in AXES]

    def beside(axis, step):
        return {AXES[axis]: lax.rem(me[axis] + step + size[axis], size[axis])}

    barrier = pltpu.get_barrier_semaphore()
    for axis in range(3):
        for step in (-1, 1):
            pl.semaphore_signal(barrier, inc=1, device_id=beside(axis, step), device_id_type=MESH)

    loads = [
        pltpu.make_async_copy(src, dst, local.at[k])
        for k, (src, dst) in enumerate(((x_hbm, x_ref), (kin_hbm, kin_ref), (grad_hbm, grad_ref)))
    ]
    for load in loads:
        load.start()

    def send(src, dst, ssem, rsem, axis, step):
        copy = pltpu.make_async_remote_copy(
            src_ref=src, dst_ref=dst, send_sem=ssem, recv_sem=rsem,
            device_id=beside(axis, step), device_id_type=MESH,
        )
        copy.start()
        return copy

    steps = (-1, 1)
    first = (0, CELLS - BUF)

    flat[...] = jnp.zeros_like(flat)
    flat[:, :CELLS] = pot_ref[...].reshape(INNER, CELLS)
    pot_s[...] = jnp.zeros_like(pot_s)
    xs[:, 384:392, :] = jnp.zeros((2, 8, 128), F32)
    for h in range(2):
        spread = flat[pl.ds(8 * h, CELLS, stride=CELLS), :]
        for m in range(1, 8):
            spread = spread + pltpu.roll(flat[pl.ds(8 * h + m, CELLS, stride=CELLS), :], CELLS * m, 1)
        pot_s[h, BUF : BUF + CELLS, :] = spread
        for side in range(2):
            xs[side, 384 + 4 * h : 387 + 4 * h, :] = pot_s[h, BUF + first[side] : 2 * BUF + first[side], :]
    loads[0].wait()
    for side in range(2):
        for j in range(BUF):
            xs[side, j * 128 : (j + 1) * 128, :] = jnp.concatenate(
                [x_ref[first[side] + j, :8].reshape(128, ORB), x_ref[first[side] + j, 8:].reshape(128, ORB)], axis=1
            )
    for i in range(OWN):
        cells[i, :INNER, :] = jnp.concatenate([x_ref[i].reshape(INNER, ORB), x_ref[OWN + i].reshape(INNER, ORB)], axis=1)

    def z_layers(p):
        for side in range(2):
            for h in range(BUF):
                zs[side, p, h * CELLS : (h + 1) * CELLS, :] = cells[p, pl.ds(first[side] + h, CELLS, stride=CELLS), :]

    def corners(p):
        for side in range(2):
            for h in range(BUF):
                cs[side, p, h * 8 : h * 8 + 6, :] = cells[p, pl.ds(ZLO + first[side] + h, 6, stride=CELLS), :]

    @pl.loop(0, OWN)
    def _(i):
        z_layers(i)

    cs[...] = jnp.zeros_like(cs)
    part = lax.broadcasted_iota(jnp.int32, (128, 128), 0)
    point = jnp.where(part < 96, lax.rem(part, 32), -1)
    halves = left_lanes(128)
    for p in range(POT):
        wanted = jnp.where(halves, BUF + p if p < OWN else p - OWN, HALF + p)
        spread_ref[:, p * 128 : (p + 1) * 128] = jnp.where(point == wanted, 1.0, 0.0).astype(BF16)
    pl.semaphore_wait(barrier, 6)

    def send_y(k, start, count):
        return [
            send(
                cells.at[pl.ds(start, count), pl.ds((0, 208)[side], 48), :],
                cells.at[pl.ds(start, count), pl.ds((YHI, YLO)[side], 48), :],
                ysend.at[side, k], yrecv.at[side, k], 1, steps[side],
            )
            for side in range(2)
        ]

    def send_z(k, start, count):
        return [
            send(
                zs.at[side, pl.ds(start, count)],
                cells.at[pl.ds(start, count), pl.ds((ZHI, ZLO)[side], 48), :],
                zsend.at[side, k], zrecv.at[side, k], 2, steps[side],
            )
            for side in range(2)
        ]

    def send_c(k, start, count):
        return [
            send(
                cs.at[side, pl.ds(start, count)],
                cells.at[pl.ds(start, count), pl.ds((CHI, CLO)[side], 24), :],
                csend.at[side, k], crecv.at[side, k], 1, steps[side],
            )
            for side in range(2)
        ]

    xcopies = []
    for j, (start, count) in enumerate(CHUNKS):
        xcopies.append([
            send(
                xs.at[side, pl.ds(start, count)], xr.at[side, pl.ds(start, count)],
                xsend.at[side, j], xrecv.at[side, j], 0, steps[side],
            )
            for side in range(2)
        ])
    ycopies = [send_y(0, 0, OWN)]
    zcopies = [send_z(0, 0, OWN)]
    ccopies = []

    def arrived(copies):
        for copy in copies:
            copy.wait_recv()

    def kinetic_part(planes, part, add):
        rows = slice(0, INNER) if part == 0 else slice(INNER, ROWS)
        cols = slice(0, 3 * INNER) if part == 0 else slice(3 * INNER, 3 * ROWS)

        def body(g):
            pair = jnp.concatenate([cells[2 * g, rows, :], cells[2 * g + 1, rows, :]], axis=1)
            done = matmul(kin_ref[:, cols], stacked(pair))
            work[2 * g] = work[2 * g] + done[:, :128] if add else done[:, :128]
            work[2 * g + 1] = work[2 * g + 1] + done[:, 128:] if add else done[:, 128:]

        pl.loop(planes[0], planes[1])(body)

    loads[1].wait()
    kinetic_part((0, OWN // 2), 0, False)
    keep = left_lanes(128)
    for j in range(BUF):
        arrived(xcopies[j])
        low = xr[1, j * 128 : (j + 1) * 128, :]
        high = xr[0, j * 128 : (j + 1) * 128, :]
        cells[HALO + j, 0:128, :] = jnp.where(keep, low, swap(high))
        cells[HALO + j, 128:256, :] = jnp.where(keep, swap(low), high)
        z_layers(HALO + j)
        if j == BUF - 1:
            for h in range(2):
                pot_s[h, 0:BUF, :] = xr[1, 384 + 4 * h : 387 + 4 * h, :]
                pot_s[h, BUF + CELLS : EXT, :] = xr[0, 384 + 4 * h : 387 + 4 * h, :]
                part = jnp.concatenate([pot_s[h], jnp.zeros((104, 128), F32)], axis=0)
                cells[POT, h * 128 : (h + 1) * 128, :] = part.T
            z_layers(POT)
        count = 2 if j == BUF - 1 else 1
        zcopies.append(send_z(1 + j, HALO + j, count))
        ycopies.append(send_y(1 + j, HALO + j, count))

    keep8 = left_lanes(8)
    sign = jnp.where(keep8, 1.0, -1.0).astype(F32)

    def load_pairs(planes):
        return [
            jnp.where(keep8, planes[HALO + a] if a < BUF else planes[a - BUF], planes[a] if a < OWN else planes[a])
            for a in range(HALF)
        ]

    def mix(pairs):
        return [swap(v) + sign * v for v in pairs]

    def unmix(total):
        return swap(total) + sign * total

    def fold(mixed):
        return (
            [mixed[b] + mixed[10 - b] for b in range(5)], [mixed[b] - mixed[10 - b] for b in range(5)], mixed[5],
        )

    def dot(coefs, values):
        total = coefs[0] * values[0]
        for c, v in zip(coefs[1:], values[1:]):
            total = total + c * v
        return total

    def table(ref, keys):
        return lambda *key: ref[keys[key] * 8 : keys[key] * 8 + 8, :]

    two, one = table(two_ref, KEYS_TWO), table(one_ref, KEYS_ONE)

    def second_along_x(pairs):
        even, odd, middle = fold(mix(pairs))
        out = [None] * HALF
        for a in range(5):
            near = dot([two("e", min(a, b), max(a, b)) for b in range(5)] + [two("m", 5 - a)], even + [middle])
            far = dot([two("o", min(a, b), max(a, b)) for b in range(5)], odd)
            out[a], out[10 - a] = unmix(near + far), unmix(near - far)
        out[5] = unmix(dot([two("m", 5 - b) for b in range(6)], even + [middle]))
        return out

    def first_along_x(pairs, wanted):
        even, odd, middle = fold(mix(pairs))
        out = [None] * HALF
        for a in range(5):
            if a not in wanted and 10 - a not in wanted:
                continue
            near = dot([one("q", b, a) for b in range(5)] + [one("m", 5 - a)], even + [middle])
            far = dot([one("q", a, b) for b in range(5)], odd)
            out[a] = unmix(far - near) if a in wanted else None
            out[10 - a] = unmix(far + near) if 10 - a in wanted else None
        if 5 in wanted:
            out[5] = unmix(dot([one("m", 5 - b) for b in range(5)], odd))
        return out

    def to_planes(pairs):
        own = [jnp.where(keep8, pairs[i + BUF], pairs[i]) for i in range(OWN)]
        return own + [jnp.where(keep8, pairs[j], pairs[OWN + j]) for j in range(BUF)]

    def tiles(start, stop, body):
        @pl.loop(start // 16, stop // 16)
        def _(r):
            for k in range(2):
                body(pl.ds(pl.multiple_of(r * 16 + k * 8, 8), 8))

    def spread_pot(rows):
        column = cells[POT, rows, :]
        high = column.astype(BF16).astype(F32)
        rest = column - high
        middle = rest.astype(BF16).astype(F32)
        parts = high + pltpu.roll(middle, 32, 1) + pltpu.roll(rest - middle, 64, 1)
        done = matmul(parts.astype(BF16), spread_ref[...])
        for p in range(POT):
            pots[p, rows, :] = done[:, p * 128 : (p + 1) * 128]

    def first_x(rows):
        planes = [cells[p, rows, :] for p in range(POT)]
        moved = to_planes(second_along_x(load_pairs(planes)))
        for p in range(POT):
            work[p, rows, :] = work[p, rows, :] + (moved[p] + (pots[p, rows, :] - center) * planes[p])

    kinetic_part((OWN // 2, PLANES // 2), 0, False)
    spread_pot(slice(0, INNER))
    tiles(0, INNER, first_x)

    arrived(zcopies[0])

    @pl.loop(0, OWN)
    def _(i):
        corners(i)

    ccopies.append(send_c(0, 0, OWN))
    for j in range(BUF):
        arrived(zcopies[1 + j])
        corners(HALO + j)
    corners(POT)
    ccopies.append(send_c(1, HALO, PLANES - HALO))
    for copies in ycopies:
        arrived(copies)
    spread_pot(slice(INNER, CROSS))
    tiles(INNER, CROSS, first_x)
    arrived(ccopies[0])
    kinetic_part((0, OWN // 2), 1, True)
    arrived(ccopies[1])
    spread_pot(slice(CROSS, ROWS))
    tiles(CROSS, ROWS, first_x)
    kinetic_part((OWN // 2, PLANES // 2), 1, True)

    def pair_of(ref, g, rows):
        return jnp.concatenate([ref[2 * g, :rows, :], ref[2 * g + 1, :rows, :]], axis=1)

    @pl.loop(0, PLANES // 2)
    def _(g):
        done = (alpha * beta) * matmul(kin_ref[:INNER, :], both_stacked(pair_of(work, g, ROWS)))
        filt[2 * g, :INNER, :] = done[:, :128]
        filt[2 * g + 1, :INNER, :] = done[:, 128:]

    def second_x(rows, count):
        planes = [work[p, rows, :] for p in range(POT)]
        moved = to_planes(second_along_x(load_pairs(planes)))
        values = []
        for p in range(count):
            applied = moved[p] + (pots[p, rows, :] - center) * planes[p]
            value = filt[p, rows, :] + ((alpha * beta) * applied - gamma * cells[p, rows, :])
            filt[p, rows, :] = value
            values.append(value)
        return values

    def inner_x(rows):
        values = second_x(rows, POT)
        slopes = first_along_x(load_pairs(values), (BUF, OWN - 1))
        low, high = slopes[BUF], slopes[OWN - 1]
        faces[0, rows, :] = jnp.where(keep8, values[0], swap(low))
        faces[1, rows, :] = jnp.where(keep8, swap(values[OWN - 1]), high)

    tiles(0, INNER, inner_x)
    fcopies = [None] * 6

    def send_faces(axis):
        fcopies[2 * axis] = send(faces.at[2 * axis], others.at[2 * axis + 1], fsend.at[2 * axis], frecv.at[2 * axis + 1], axis, -1)
        fcopies[2 * axis + 1] = send(faces.at[2 * axis + 1], others.at[2 * axis], fsend.at[2 * axis + 1], frecv.at[2 * axis], axis, 1)

    send_faces(0)

    @pl.loop(0, OWN // 2)
    def _(g):
        done = (alpha * beta) * matmul(kin_ref[INNER:CROSS, :], both_stacked(pair_of(work, g, ROWS)))
        filt[2 * g, INNER:CROSS, :] = done[:, :128]
        filt[2 * g + 1, INNER:CROSS, :] = done[:, 128:]

    def outer_x(rows):
        second_x(rows, OWN)

    tiles(INNER, CROSS, outer_x)

    loads[2].wait()

    @pl.loop(0, OWN // 2)
    def _(g):
        done = matmul(grad_ref[...], both_stacked(pair_of(filt, g, CROSS)))
        gyz[2 * g] = done[:, :128]
        gyz[2 * g + 1] = done[:, 128:]

    keep16 = left_lanes(16)
    for i in range(OWN):
        for side, layer in ((0, 0), (1, CELLS - 1)):
            for f, value, deriv in (
                (2 + side, filt[i, layer * 16 : layer * 16 + 16, :], gyz[i, layer * 16 : layer * 16 + 16, :]),
                (4 + side, filt[i, pl.ds(layer, 16, stride=16), :], gyz[i, pl.ds(INNER + layer, 16, stride=16), :]),
            ):
                faces[f, i * 16 : i * 16 + 16, :] = jnp.where(keep16, value, swap(deriv))
                faces[f, 128 + i * 16 : 144 + i * 16, :] = jnp.where(keep16, swap(value), deriv)
    send_faces(1)
    send_faces(2)

    def full_gx(rows):
        planes = [filt[p, rows, :] for p in range(POT)]
        moved = first_along_x(load_pairs(planes), range(HALF))
        for i in range(OWN):
            gx[i, rows, :] = jnp.where(keep8, moved[i + BUF], moved[i])

    tiles(0, INNER, full_gx)
    basis_ref[...] = filt[:OWN, :INNER, :]

    def volume(i, total):
        value = filt[i, :INNER, :]
        left, left_low = split(value)
        right, right_low = split(2.0 * pots[i, :INNER, :] * value)
        slopes = [split(part) for part in (gx[i], gyz[i, :INNER, :], gyz[i, INNER:, :])]
        lefts = [left] + [high for high, _ in slopes]
        rights = [right] + [high for high, _ in slopes] + [right_low] + [2.0 * low for _, low in slopes] + [right]
        return total + gram(jnp.concatenate(lefts + lefts + [left_low], axis=0), jnp.concatenate(rights, axis=0))

    total = lax.fori_loop(0, OWN, volume, jnp.zeros((128, 128), F32))
    total = 0.25 * (total + total.T)
    diagonal = total[:ORB, :ORB] + total[ORB:, ORB:]
    for f in range(6):
        s = -1.0 if f % 2 == 0 else 1.0
        pair = split(faces[f])
        own = gram_split(pair, pair)
        diagonal = diagonal - (0.25 * s) * (own[:ORB, ORB:] + own[ORB:, :ORB]) + (0.5 * PENALTY) * own[:ORB, :ORB]
    blocks_ref[0] = diagonal
    for f in (2, 3, 4, 5, 0, 1):
        fcopies[f ^ 1].wait_recv()
        s = -1.0 if f % 2 == 0 else 1.0
        both = gram_split(split(faces[f]), split(others[f]))
        blocks_ref[1 + f] = (0.25 * s) * (both[ORB:, :ORB] - both[:ORB, ORB:]) - (0.5 * PENALTY) * both[:ORB, :ORB]
    for copies in xcopies + ycopies + zcopies + ccopies + [fcopies]:
        for copy in copies:
            copy.wait_send()


def unpack_kernel(packed_ref, blocks_in, basis_ref, blocks_ref):
    blocks_ref[...] = blocks_in[...]
    for i in range(OWN):
        value = packed_ref[i]
        basis_ref[i] = value[:, :ORB].reshape(CELLS, CELLS, ORB)
        basis_ref[OWN + i] = swap(value)[:, :ORB].reshape(CELLS, CELLS, ORB)


def on_device(orbitals, potential):
    kinetic, gradient = plane_matrices()
    vmem = pl.BlockSpec(memory_space=pltpu.VMEM)
    hbm = pl.BlockSpec(memory_space=pl.ANY)
    dma = pltpu.SemaphoreType.DMA
    blocks_shape = jax.ShapeDtypeStruct((7, ORB, ORB), F32)
    tables = [jnp.asarray(np.repeat(t, 8, axis=0), F32) for t in (SECOND, FIRST)]
    packed, blocks = pl.pallas_call(
        kernel,
        out_shape=(jax.ShapeDtypeStruct((OWN, INNER, 128), F32), blocks_shape),
        in_specs=[hbm, vmem, hbm, hbm, vmem, vmem],
        out_specs=(vmem, vmem),
        scratch_shapes=[
            pltpu.VMEM((CELLS, CELLS, CELLS, ORB), F32),
            pltpu.VMEM(kinetic.shape, BF16),
            pltpu.VMEM(gradient.shape, BF16),
            pltpu.VMEM((128, POT * 128), BF16),
            pltpu.VMEM((2, MESSAGE, 128), F32),
            pltpu.VMEM((2, MESSAGE, 128), F32),
            pltpu.VMEM((INNER, 128), F32),
            pltpu.VMEM((2, 24, 128), F32),
            pltpu.VMEM((PLANES, ROWS, 128), F32),
            pltpu.VMEM((POT, ROWS, 128), F32),
            pltpu.VMEM((PLANES, ROWS, 128), F32),
            pltpu.VMEM((PLANES, CROSS, 128), F32),
            pltpu.VMEM((2, PLANES, 48, 128), F32),
            pltpu.VMEM((2, PLANES, 24, 128), F32),
            pltpu.VMEM((OWN, INNER, 128), F32),
            pltpu.VMEM((OWN, 2 * INNER, 128), F32),
            pltpu.VMEM((6, INNER, 128), F32),
            pltpu.VMEM((6, INNER, 128), F32),
            dma((3,)),
            dma((2, 3)), dma((2, 3)), dma((2, 4)), dma((2, 4)), dma((2, 4)), dma((2, 4)),
            dma((2, 2)), dma((2, 2)), dma((6,)), dma((6,)),
        ],
        compiler_params=pltpu.CompilerParams(
            collective_id=0, has_side_effects=True, vmem_limit_bytes=60 * 1024 * 1024
        ),
    )(orbitals, potential, kinetic, gradient, *tables)
    basis, blocks = pl.pallas_call(
        unpack_kernel,
        out_shape=(jax.ShapeDtypeStruct((CELLS, CELLS, CELLS, ORB), F32), blocks_shape),
        in_specs=[vmem, vmem],
        out_specs=(vmem, vmem),
    )(packed, blocks)
    return basis, blocks[None, None, None]


def solution(mesh):
    return jax.shard_map(
        on_device,
        mesh=mesh,
        in_specs=(P("gx", "gy", "gz", None), P("gx", "gy", "gz")),
        out_specs=(P("gx", "gy", "gz", None), P("gx", "gy", "gz", None, None, None)),
        check_vma=False,
    )
```

time: 115 us -> 79.8 us (0.69)
  the two profiles are of different devices: /device:TPU:17 before, /device:TPU:1 now
where the time goes in v2:
time: 79.8 us; the launch traced here: 79.6 us
  Pallas kernels  79 us (99%)
    pallas_call x1, Pallas kernels, on_device(): pl.pallas_call(kernel, out_shape=(jax.ShapeDtypeStruct((OWN, INNER, 128),...  76.1 us
    pallas_call x1, Pallas kernels, on_device(): pl.pallas_call(unpack_kernel, out_shape=(jax.ShapeDtypeStruct((CELLS, CEL...  2.92 us

profile of v2, /device:TPU:1, one launch (start us, length us, event | category | flops | bytes accessed | tf_op | source)
XLA Modules:
  0.0 79.6 jit_solution(8204791603094227051)
XLA Ops:
  0.6 76.1 %shard_map.77 = (f32[8,256,128]{2,1,0:T(8,128)}, f32[7,64,64]{2,1,0:T(8,128)}) custom-call(f32[16,16,16,64]{3,2,1,0:T(8,128)} %x_hbm.1, f32[16,16,16]{2,1,0:T(8,128)} %pot_ref.1, bf16[496,1488]{1,0:T(8,128)(2,1)} %constant.20.kin_hbm, bf16[512,1344]{1,0:T(8,128)(2,1)} %constant.29.grad_hbm, f32[288,128]{1,0:T(8,128)} %constant.10.clone.two_ref, ...), custom_call_target="tpu_custom_call" | custom-call | tf_op jit(solution)/shard_map/pallas_call | solution.py:551
  76.7 2.9 %shard_map.78 = (f32[16,16,16,64]{3,2,1,0:T(8,128)}, f32[7,64,64]{2,1,0:T(8,128)}) custom-call(f32[8,256,128]{2,1,0:T(8,128)} %get-tuple-element.6.packed_ref, f32[7,64,64]{2,1,0:T(8,128)} %get-tuple-element.7.blocks_in), custom_call_target="tpu_custom_call" | custom-call | tf_op jit(solution)/shard_map/pallas_call | solution.py:583

commit v3 on v2

--- a/solution.py
+++ b/solution.py
@@ -164,9 +164,9 @@
 def kernel(
     x_hbm, pot_ref, kin_hbm, grad_hbm, two_ref, one_ref,
     basis_ref, blocks_ref,
-    x_ref, kin_ref, grad_ref, spread_ref,
+    x_ref, kin_ref, grad_ref, spread_ref, done_ref, rest_ref, mids, backs, bundle,
     xs, xr, flat, pot_s, cells, pots, work, filt, zs, cs, gx, gyz, faces, others,
-    local, xsend, xrecv, ysend, yrecv, zsend, zrecv, csend, crecv, fsend, frecv,
+    local, xsend, xrecv, ysend, yrecv, zsend, zrecv, csend, crecv, fsend, frecv, msend, mrecv,
 ):
     center, alpha, beta, gamma = cheb_constants()
     me = [lax.axis_index(a) for a in AXES]
@@ -175,10 +175,31 @@
     def beside(axis, step):
         return {AXES[axis]: lax.rem(me[axis] + step + size[axis], size[axis])}
 
+    ring = size[2]
+    reach = ring // 4
+
+    def along_y(gx, gz, step):
+        position = lax.rem(lax.rem(gx, 2) * (ring // 2) + gz // 2 + step + ring, ring)
+        return (
+            gx // 2 * 2 + position // (ring // 2),
+            lax.rem(position, ring // 2) * 2 + lax.rem(gz, 2),
+        )
+
+    def device(gx, gz):
+        return {AXES[0]: gx, AXES[2]: gz}
+
+    below = lax.rem(me[0] + size[0] - 1, size[0])
+    upper_mid = device(*along_y(me[0], me[2], reach))
+    lower_mid = device(*along_y(below, me[2], reach))
+    served_gx, served_gz = along_y(me[0], me[2], -reach)
+    served = device(served_gx, served_gz)
+    served_next = device(lax.rem(served_gx + 1, size[0]), served_gz)
+
     barrier = pltpu.get_barrier_semaphore()
-    for axis in range(3):
-        for step in (-1, 1):
-            pl.semaphore_signal(barrier, inc=1, device_id=beside(axis, step), device_id_type=MESH)
+    partners = [beside(axis, step) for axis in range(3) for step in (-1, 1)]
+    partners += [upper_mid, lower_mid, served, served_next]
+    for partner in partners:
+        pl.semaphore_signal(barrier, inc=1, device_id=partner, device_id_type=MESH)
 
     loads = [
         pltpu.make_async_copy(src, dst, local.at[k])
@@ -187,13 +208,15 @@
     for load in loads:
         load.start()
 
-    def send(src, dst, ssem, rsem, axis, step):
+    def send_to(src, dst, ssem, rsem, target):
         copy = pltpu.make_async_remote_copy(
-            src_ref=src, dst_ref=dst, send_sem=ssem, recv_sem=rsem,
-            device_id=beside(axis, step), device_id_type=MESH,
+            src_ref=src, dst_ref=dst, send_sem=ssem, recv_sem=rsem, device_id=target, device_id_type=MESH,
         )
         copy.start()
         return copy
+
+    def send(src, dst, ssem, rsem, axis, step):
+        return send_to(src, dst, ssem, rsem, beside(axis, step))
 
     steps = (-1, 1)
     first = (0, CELLS - BUF)
@@ -239,7 +262,7 @@
     for p in range(POT):
         wanted = jnp.where(halves, BUF + p if p < OWN else p - OWN, HALF + p)
         spread_ref[:, p * 128 : (p + 1) * 128] = jnp.where(point == wanted, 1.0, 0.0).astype(BF16)
-    pl.semaphore_wait(barrier, 6)
+    pl.semaphore_wait(barrier, 10)
 
     def send_y(k, start, count):
         return [
@@ -380,11 +403,14 @@
         own = [jnp.where(keep8, pairs[i + BUF], pairs[i]) for i in range(OWN)]
         return own + [jnp.where(keep8, pairs[j], pairs[OWN + j]) for j in range(BUF)]
 
+    def tile(r):
+        return pl.ds(pl.multiple_of(r * 8, 8), 8)
+
     def tiles(start, stop, body):
         @pl.loop(start // 16, stop // 16)
         def _(r):
             for k in range(2):
-                body(pl.ds(pl.multiple_of(r * 16 + k * 8, 8), 8))
+                body(tile(2 * r + k))
 
     def spread_pot(rows):
         column = cells[POT, rows, :]
@@ -432,49 +458,56 @@
     def pair_of(ref, g, rows):
         return jnp.concatenate([ref[2 * g, :rows, :], ref[2 * g + 1, :rows, :]], axis=1)
 
+    def second_x(rows):
+        planes = [work[p, rows, :] for p in range(POT)]
+        moved = to_planes(second_along_x(load_pairs(planes)))
+        return [
+            (alpha * beta) * (moved[p] + (pots[p, rows, :] - center) * planes[p]) - gamma * cells[p, rows, :]
+            for p in range(POT)
+        ]
+
     @pl.loop(0, PLANES // 2)
     def _(g):
         done = (alpha * beta) * matmul(kin_ref[:INNER, :], both_stacked(pair_of(work, g, ROWS)))
-        filt[2 * g, :INNER, :] = done[:, :128]
-        filt[2 * g + 1, :INNER, :] = done[:, 128:]
-
-    def second_x(rows, count):
-        planes = [work[p, rows, :] for p in range(POT)]
-        moved = to_planes(second_along_x(load_pairs(planes)))
-        values = []
-        for p in range(count):
-            applied = moved[p] + (pots[p, rows, :] - center) * planes[p]
-            value = filt[p, rows, :] + ((alpha * beta) * applied - gamma * cells[p, rows, :])
-            filt[p, rows, :] = value
-            values.append(value)
-        return values
-
-    def inner_x(rows):
-        values = second_x(rows, POT)
-        slopes = first_along_x(load_pairs(values), (BUF, OWN - 1))
-        low, high = slopes[BUF], slopes[OWN - 1]
-        faces[0, rows, :] = jnp.where(keep8, values[0], swap(low))
-        faces[1, rows, :] = jnp.where(keep8, swap(values[OWN - 1]), high)
-
-    tiles(0, INNER, inner_x)
-    fcopies = [None] * 6
-
-    def send_faces(axis):
-        fcopies[2 * axis] = send(faces.at[2 * axis], others.at[2 * axis + 1], fsend.at[2 * axis], frecv.at[2 * axis + 1], axis, -1)
-        fcopies[2 * axis + 1] = send(faces.at[2 * axis + 1], others.at[2 * axis], fsend.at[2 * axis + 1], frecv.at[2 * axis], axis, 1)
-
-    send_faces(0)
+        done_ref[2 * g] = done[:, :128]
+        done_ref[2 * g + 1] = done[:, 128:]
+        for k in range(6):
+            rows = tile(6 * g + k)
+            for p, value in enumerate(second_x(rows)):
+                filt[p, rows, :] = value
 
     @pl.loop(0, OWN // 2)
     def _(g):
         done = (alpha * beta) * matmul(kin_ref[INNER:CROSS, :], both_stacked(pair_of(work, g, ROWS)))
-        filt[2 * g, INNER:CROSS, :] = done[:, :128]
-        filt[2 * g + 1, INNER:CROSS, :] = done[:, 128:]
-
-    def outer_x(rows):
-        second_x(rows, OWN)
-
-    tiles(INNER, CROSS, outer_x)
+        rest_ref[2 * g] = done[:, :128]
+        rest_ref[2 * g + 1] = done[:, 128:]
+        for k in range(8):
+            rows = tile(8 * g + k)
+            values = [filt[p, rows, :] + done_ref[p, rows, :] for p in range(POT)]
+            slopes = first_along_x(load_pairs(values), (BUF, OWN - 1))
+            for p in range(POT):
+                filt[p, rows, :] = values[p]
+            faces[0, rows, :] = jnp.where(keep8, values[0], swap(slopes[BUF]))
+            faces[1, rows, :] = jnp.where(keep8, swap(values[OWN - 1]), slopes[OWN - 1])
+
+    fcopies = [
+        send_to(faces.at[0], mids.at[1], fsend.at[0], frecv.at[0], lower_mid),
+        send_to(faces.at[1], mids.at[0], fsend.at[1], frecv.at[1], upper_mid),
+    ]
+    result = pltpu.make_async_copy(filt.at[pl.ds(0, OWN), pl.ds(0, INNER), :], basis_ref, local.at[3])
+    result.start()
+
+    for i in range(OWN):
+        filt[i, INNER : INNER + 32, :] = filt[i, INNER : INNER + 32, :] + rest_ref[i, :32, :]
+
+    @pl.loop(18, CROSS // 16)
+    def _(r):
+        for k in range(2):
+            rows = tile(2 * r + k)
+            shifted = tile(2 * r + k - INNER // 8)
+            values = second_x(rows)
+            for i in range(OWN):
+                filt[i, rows, :] = values[i] + rest_ref[i, shifted, :]
 
     loads[2].wait()
 
@@ -483,6 +516,11 @@
         done = matmul(grad_ref[...], both_stacked(pair_of(filt, g, CROSS)))
         gyz[2 * g] = done[:, :128]
         gyz[2 * g + 1] = done[:, 128:]
+        for k in range(8):
+            rows = tile(8 * g + k)
+            moved = first_along_x(load_pairs([filt[p, rows, :] for p in range(POT)]), range(HALF))
+            for i in range(OWN):
+                gx[i, rows, :] = jnp.where(keep8, moved[i + BUF], moved[i])
 
     keep16 = left_lanes(16)
     for i in range(OWN):
@@ -493,52 +531,78 @@
             ):
                 faces[f, i * 16 : i * 16 + 16, :] = jnp.where(keep16, value, swap(deriv))
                 faces[f, 128 + i * 16 : 144 + i * 16, :] = jnp.where(keep16, swap(value), deriv)
-    send_faces(1)
-    send_faces(2)
-
-    def full_gx(rows):
-        planes = [filt[p, rows, :] for p in range(POT)]
-        moved = first_along_x(load_pairs(planes), range(HALF))
-        for i in range(OWN):
-            gx[i, rows, :] = jnp.where(keep8, moved[i + BUF], moved[i])
-
-    tiles(0, INNER, full_gx)
-    basis_ref[...] = filt[:OWN, :INNER, :]
+    for axis in (1, 2):
+        for side in range(2):
+            f = 2 * axis + side
+            fcopies.append(send(faces.at[f], others.at[f ^ 1], fsend.at[f], frecv.at[f ^ 1], axis, steps[side]))
 
     def volume(i, total):
         value = filt[i, :INNER, :]
         left, left_low = split(value)
         right, right_low = split(2.0 * pots[i, :INNER, :] * value)
         slopes = [split(part) for part in (gx[i], gyz[i, :INNER, :], gyz[i, INNER:, :])]
-        lefts = [left] + [high for high, _ in slopes]
-        rights = [right] + [high for high, _ in slopes] + [right_low] + [2.0 * low for _, low in slopes] + [right]
-        return total + gram(jnp.concatenate(lefts + lefts + [left_low], axis=0), jnp.concatenate(rights, axis=0))
-
-    total = lax.fori_loop(0, OWN, volume, jnp.zeros((128, 128), F32))
+        lefts = jnp.concatenate([left] + [high for high, _ in slopes], axis=0)
+        rights = jnp.concatenate([right] + [high for high, _ in slopes], axis=0)
+        lows = jnp.concatenate([right_low] + [2.0 * low for _, low in slopes], axis=0)
+        many = gram(lefts, jnp.concatenate([rights, lows], axis=1))
+        return total + (many[:, :128] + many[:, 128:]) + gram(left_low, right)
+
+    keep256 = left_lanes(256)
+
+    def product(face, right):
+        high, low = split(face)
+        right_high, right_low = split(right)
+        width = right.shape[1]
+        many = gram(high, jnp.concatenate([right_high, right_low], axis=1))
+        return many[:, :width] + many[:, width:] + gram(low, right_high)
+
+    def coupling_right(other, s):
+        flipped = swap(other)
+        return jnp.where(keep256, (-0.5 * PENALTY) * other - (0.25 * s) * flipped, (0.25 * s) * flipped)
+
+    def own_right(face, s):
+        return jnp.where(keep256, (0.25 * PENALTY) * face - (0.25 * s) * swap(face), 0.0)
+
+    total = lax.fori_loop(0, 5, volume, jnp.zeros((128, 128), F32))
+
+    fcopies[0].wait_recv()
+    fcopies[1].wait_recv()
+    both = product(mids[0], coupling_right(mids[1], 1.0))
+    block = both[:ORB, :ORB] + both[ORB:, ORB:]
+    for side, value in ((0, block), (1, block.T)):
+        bundle[side] = jnp.concatenate([value[: ORB // 2], value[ORB // 2 :]], axis=1)
+    mcopies = [
+        send_to(bundle.at[0], backs.at[1], msend.at[0], mrecv.at[1], served),
+        send_to(bundle.at[1], backs.at[0], msend.at[1], mrecv.at[0], served_next),
+    ]
+
+    total = lax.fori_loop(5, OWN, volume, total)
     total = 0.25 * (total + total.T)
     diagonal = total[:ORB, :ORB] + total[ORB:, ORB:]
-    for f in range(6):
-        s = -1.0 if f % 2 == 0 else 1.0
-        pair = split(faces[f])
-        own = gram_split(pair, pair)
-        diagonal = diagonal - (0.25 * s) * (own[:ORB, ORB:] + own[ORB:, :ORB]) + (0.5 * PENALTY) * own[:ORB, :ORB]
-    blocks_ref[0] = diagonal
-    for f in (2, 3, 4, 5, 0, 1):
-        fcopies[f ^ 1].wait_recv()
-        s = -1.0 if f % 2 == 0 else 1.0
-        both = gram_split(split(faces[f]), split(others[f]))
-        blocks_ref[1 + f] = (0.25 * s) * (both[ORB:, :ORB] - both[:ORB, ORB:]) - (0.5 * PENALTY) * both[:ORB, :ORB]
-    for copies in xcopies + ycopies + zcopies + ccopies + [fcopies]:
+    halves = jnp.zeros((128, 128), F32)
+    for f in range(2):
+        halves = halves + product(faces[f], own_right(faces[f], 2.0 * f - 1.0))
+    for f in range(2, 6):
+        fcopies[f].wait_recv()
+
+    def face_terms(f, halves):
+        s = 2.0 * lax.rem(f, 2).astype(F32) - 1.0
+        right = jnp.concatenate([coupling_right(others[f], s), own_right(faces[f], s)], axis=1)
+        both = product(faces[f], right)
+        blocks_ref[1 + f] = both[:ORB, :ORB] + both[ORB:, ORB:128]
+        return halves + both[:, 128:]
+
+    halves = lax.fori_loop(2, 6, face_terms, halves)[:ORB, :ORB]
+    blocks_ref[0] = diagonal + (halves + halves.T)
+    for side in range(2):
+        mcopies[1 - side].wait_recv()
+        got = backs[side]
+        blocks_ref[1 + side, : ORB // 2, :] = got[:, :ORB]
+        blocks_ref[1 + side, ORB // 2 :, :] = swap(got)[:, :ORB]
+    result.wait()
+    for copies in xcopies + ycopies + zcopies + ccopies + [fcopies, mcopies]:
         for copy in copies:
             copy.wait_send()
-
-
-def unpack_kernel(packed_ref, blocks_in, basis_ref, blocks_ref):
-    blocks_ref[...] = blocks_in[...]
-    for i in range(OWN):
-        value = packed_ref[i]
-        basis_ref[i] = value[:, :ORB].reshape(CELLS, CELLS, ORB)
-        basis_ref[OWN + i] = swap(value)[:, :ORB].reshape(CELLS, CELLS, ORB)
 
 
 def on_device(orbitals, potential):
@@ -552,12 +616,17 @@
         kernel,
         out_shape=(jax.ShapeDtypeStruct((OWN, INNER, 128), F32), blocks_shape),
         in_specs=[hbm, vmem, hbm, hbm, vmem, vmem],
-        out_specs=(vmem, vmem),
+        out_specs=(hbm, vmem),
         scratch_shapes=[
             pltpu.VMEM((CELLS, CELLS, CELLS, ORB), F32),
             pltpu.VMEM(kinetic.shape, BF16),
             pltpu.VMEM(gradient.shape, BF16),
             pltpu.VMEM((128, POT * 128), BF16),
+            pltpu.VMEM((PLANES, INNER, 128), F32),
+            pltpu.VMEM((OWN, CROSS - INNER, 128), F32),
+            pltpu.VMEM((2, INNER, 128), F32),
+            pltpu.VMEM((2, ORB // 2, 128), F32),
+            pltpu.VMEM((2, ORB // 2, 128), F32),
             pltpu.VMEM((2, MESSAGE, 128), F32),
             pltpu.VMEM((2, MESSAGE, 128), F32),
             pltpu.VMEM((INNER, 128), F32),
@@ -572,20 +641,15 @@
             pltpu.VMEM((OWN, 2 * INNER, 128), F32),
             pltpu.VMEM((6, INNER, 128), F32),
             pltpu.VMEM((6, INNER, 128), F32),
-            dma((3,)),
+            dma((4,)),
             dma((2, 3)), dma((2, 3)), dma((2, 4)), dma((2, 4)), dma((2, 4)), dma((2, 4)),
-            dma((2, 2)), dma((2, 2)), dma((6,)), dma((6,)),
+            dma((2, 2)), dma((2, 2)), dma((6,)), dma((6,)), dma((2,)), dma((2,)),
         ],
         compiler_params=pltpu.CompilerParams(
             collective_id=0, has_side_effects=True, vmem_limit_bytes=60 * 1024 * 1024
         ),
     )(orbitals, potential, kinetic, gradient, *tables)
-    basis, blocks = pl.pallas_call(
-        unpack_kernel,
-        out_shape=(jax.ShapeDtypeStruct((CELLS, CELLS, CELLS, ORB), F32), blocks_shape),
-        in_specs=[vmem, vmem],
-        out_specs=(vmem, vmem),
-    )(packed, blocks)
+    basis = jnp.concatenate([packed[:, :, :ORB], packed[:, :, ORB:]], axis=0).reshape(CELLS, CELLS, CELLS, ORB)
     return basis, blocks[None, None, None]
 
 

time: 79.8 us -> 72.7 us (0.911)
  Pallas kernels: 79 us -> 67.8 us
  local copies, waits for them, and re-layouts: 0 us -> 2.6 us
  other arithmetic: 0 us -> 1.51 us
    pallas_call x1, Pallas kernels: 76.1 us -> 67.8 us  [on_device(): pl.pallas_call(kernel, out_shape=(jax.ShapeDtypeStruct((OWN, INNER, 128),...]
    pallas_call x1 -> x0, Pallas kernels: 2.92 us -> none  [on_device(): pl.pallas_call(unpack_kernel, out_shape=(jax.ShapeDtypeStruct((CELLS, CEL...]
    slice x0 -> x1, local copies, waits for them, and re-layouts: none -> 1.91 us  [on_device(): packed[:, :, :ORB]]
    concatenate x0 -> x1, other arithmetic: none -> 1.51 us  [on_device(): jnp.concatenate([packed[:, :, :ORB], packed[:, :, ORB:]], axis=0)]
where the time goes in v3:
time: 72.7 us; the launch traced here: 72.6 us
  Pallas kernels  67.8 us (93%)
  local copies, waits for them, and re-layouts  2.6 us (4%)
  other arithmetic  1.51 us (2%)
    pallas_call x1, Pallas kernels, on_device(): pl.pallas_call(kernel, out_shape=(jax.ShapeDtypeStruct((OWN, INNER, 128),...  67.8 us
    slice x1, local copies, waits for them, and re-layouts, on_device(): packed[:, :, :ORB]  1.91 us
    concatenate x1, other arithmetic, on_device(): jnp.concatenate([packed[:, :, :ORB], packed[:, :, ORB:]], axis=0)  1.51 us

profile of v3, /device:TPU:1, one launch (start us, length us, event | category | flops | bytes accessed | tf_op | source)
XLA Modules:
  0.0 72.6 jit_solution(3345388054027052786)
XLA Ops:
  0.6 67.8 %shard_map.77 = (f32[8,256,128]{2,1,0:T(8,128)}, f32[7,64,64]{2,1,0:T(8,128)}) custom-call(f32[16,16,16,64]{3,2,1,0:T(8,128)} %x_hbm.1, f32[16,16,16]{2,1,0:T(8,128)} %pot_ref.1, bf16[496,1488]{1,0:T(8,128)(2,1)} %constant.20.kin_hbm, bf16[512,1344]{1,0:T(8,128)(2,1)} %constant.29.grad_hbm, f32[288,128]{1,0:T(8,128)} %constant.10.clone.two_ref, ...), custom_call_target="tpu_custom_call" | custom-call | tf_op jit(solution)/shard_map/pallas_call | solution.py:615
  68.5 1.9 %fusion = (f32[8,256,64]{2,1,0:T(8,128)S(1)}, f32[8,256,64]{2,1,0:T(8,128)S(1)}) fusion(f32[8,256,128]{2,1,0:T(8,128)} %get-tuple-element.4), kind=kLoop, calls=%fused_computation.1 | loop fusion | bytes 2097152 | tf_op jit(solution)/shard_map/slice | solution.py:652
  70.4 0.0 copy-start
  70.4 1.5 %pad_maximum_fusion = f32[16,256,64]{2,1,0:T(8,128)} fusion(f32[8,256,64]{2,1,0:T(8,128)S(1)} %get-tuple-element.7, f32[8,256,64]{2,1,0:T(8,128)S(1)} %get-tuple-element.6), kind=kLoop, calls=%fused_computation | loop fusion | flops 262144 | bytes 2097152 | tf_op jit(solution)/shard_map/concatenate | solution.py:652
  71.9 0.0 copy-done
  71.9 0.7 copy.9
Async XLA Ops:
  70.4 1.5 %copy-start = (f32[7,64,64]{2,1,0:T(8,128)S(1)}, f32[7,64,64]{2,1,0:T(8,128)}, u32[]{:S(2)}) copy-start(f32[7,64,64]{2,1,0:T(8,128)} %get-tuple-element.5) | copy-start | bytes 344068
